TPU v7x, 32 devices: a whole 2x2x4 slice. The times are simulated.
32 devices in a mesh: gx: 4 (over z), gy: 4 (over y, x), gz: 2 (over core).
Axes of the slice: x: 2, y: 2, z: 4, core: 2. Of those that a mesh axis runs over, the one named last changes fastest.
Arguments:
- places: float32 [256, 3], P(('gx', 'gy', 'gz')), may hold values from 0 to 1
- scalars: float32 [256, 256], P(('gx', 'gy', 'gz')), may hold values from -6 to 6
- vectors: float32 [256, 3, 256], P(('gx', 'gy', 'gz')), may hold values from -6 to 6
- species: int32 [256], P(('gx', 'gy', 'gz')), may hold values from 0 to 3
- bound_rows: int32 [256], P(('gx', 'gy', 'gz')), may hold values from 0 to 7, as said below
- bound_count: int32 [32], P(('gx', 'gy', 'gz')), may hold values from 4 to 8, as said below
- neighbour_ids: int32 [16, 256], P(None, ('gx', 'gy', 'gz')), may hold values from 0 to 223, as said below
- neighbour_count: int32 [256], P(('gx', 'gy', 'gz')), may hold values from 3 to 16, as said below
- radial_first: bfloat16 [8, 64], replicated, may hold values from -2 to 2
- radial_second: bfloat16 [64, 64], replicated, may hold values from -0.75 to 0.75
- radial_third: bfloat16 [64, 1536], replicated, may hold values from -0.75 to 0.75
- energy_table: float32 [4, 256], replicated, may hold values from -6 to 6
- vector_gains: float32 [256], replicated, may hold values from -3 to 3
Outputs:
- atom_energy: float32 [256], P(('gx', 'gy', 'gz'))
- forces: float32 [256, 3], P(('gx', 'gy', 'gz'))
- grad_scalars: float32 [256, 256], P(('gx', 'gy', 'gz'))
- grad_vectors: float32 [256, 3, 256], P(('gx', 'gy', 'gz'))
Inputs may be any that keep to these rules, and one draw needn't show every extreme that they name: `bound_rows`: per domain, 8 distinct indices of its own atoms (0 to 7). `bound_count`: some domain has all 8 slots live. `neighbour_ids`: below 8: an owned atom other than the atom itself; otherwise 8 + t * 8 + b for ghost block t, never the centre block 13, and any slot b, live or not. `neighbour_count`: slots k below the count are listed neighbours. Domains differ in their largest count; some atom has 16.
All inputs are finite; a program needn't handle non-finite values.
Results may differ from a plain program's by a relative error of at most 0.014.
Values sent between devices are 32-bit elements; how exact they have to be, the bound alone decides.
No kernel may reach another device: no remote copies, remote signals or barrier semaphores. Data moves between devices by JAX's collectives and lax.ppermute only.
A program may use at most 64 MiB of HBM per device.

v0:
```python
import functools

import jax
import jax.numpy as jnp
from jax import lax
from jax.experimental import pallas as pl
from jax.experimental.pallas import tpu as pltpu
from jax.sharding import PartitionSpec as P


SOFTENING = 0.25
SHARPNESS = 2.0
FIRST_CENTRE = 0.5
SPACING = 0.4
EDGE = 1.0
LANES = 128
HIGHEST = lax.Precision.HIGHEST
AXES = ("gx", "gy", "gz")


def dot(a, b, dims, precision=None):
    return lax.dot_general(
        a, b, ((dims[:1], dims[1:]), ((), ())), precision=precision,
        preferred_element_type=jnp.float32,
    )


def thirds(x, axis=0):
    high = x.astype(jnp.bfloat16).astype(jnp.float32)
    rest = x - high
    middle = rest.astype(jnp.bfloat16).astype(jnp.float32)
    return jnp.concatenate([high, middle, rest - middle], axis=axis).astype(jnp.bfloat16)


def joined(x, rows):
    return x[0:rows, :] + (x[rows : 2 * rows, :] + x[2 * rows :, :])


def sides(size):
    if size == 1:
        return []
    if size == 2:
        return [[(0, 1), (1, 0)]]
    if size % 2:
        return [[((i + 1) % size, i) for i in range(size)], [(i, (i + 1) % size) for i in range(size)]]
    pairs = [[(i, (i + 1) % size) for i in range(first, size, 2)] for first in (0, 1)]
    return [half + [(b, a) for a, b in half] for half in pairs]


def backwards(pairs_list):
    return reversed(list(enumerate(pairs_list)))


def inverse(pairs):
    return [(b, a) for a, b in pairs]


def pack_kernel(
    bound_count, bound_rows_in, places_in, scalars_in, vectors_in, out,
    bound_rows, places, scalars, vectors, sems,
):
    pairs = [(bound_rows_in, bound_rows), (places_in, places), (scalars_in, scalars), (vectors_in, vectors)]
    copies = [pltpu.make_async_copy(a, b, sems.at[n]) for n, (a, b) in enumerate(pairs)]
    for copy in copies:
        copy.start()
    for copy in copies:
        copy.wait()
    boundary = bound_rows.shape[0]
    channels = scalars.shape[1]
    halves = channels // LANES
    source = lax.broadcasted_iota(jnp.int32, (places.shape[1], LANES), 0)
    lane = lax.broadcasted_iota(jnp.int32, (places.shape[1], LANES), 1)
    moved = jnp.zeros(source.shape, jnp.float32)
    for slot in range(boundary):
        atom = bound_rows[slot]
        alive = jnp.where(slot < bound_count[0], 1.0, 0.0).astype(jnp.float32)
        rows = [scalars[pl.ds(atom, 1), :]] + [vectors[a, pl.ds(atom, 1), :] for a in range(3)]
        for part, row in enumerate(rows):
            row = row * alive
            for h in range(halves):
                at = (part * halves + h) * boundary + slot
                out[at : at + 1, :] = row[:, h * LANES : (h + 1) * LANES]
        moved = jnp.where((lane == slot) & (source == atom), alive, moved)
    spots = dot(places[...], moved, (1, 0), HIGHEST)
    out[4 * halves * boundary :, :] = jnp.concatenate([spots, jnp.zeros((boundary - 3, LANES), jnp.float32)], axis=0)


def prep_kernel(
    wide, parities, ids, counts, species, energy_table, bound_rows, bound_count, *rest
):
    atoms, slots = ids.shape
    edges = atoms * slots
    f32 = jnp.float32
    count = (len(rest) - 6) // 2
    passed, (picks, contrast, displace, usable, coeff, lands), copied = rest[:count], rest[count:-count], rest[-count:]
    for a, b in zip(passed, copied):
        b[...] = a[...]
    lane = lax.broadcasted_iota(jnp.int32, (atoms, edges), 1)
    mine = lane % atoms == lax.broadcasted_iota(jnp.int32, (atoms, edges), 0)
    slot_lane = lax.broadcasted_iota(jnp.int32, (slots, edges), 1) // atoms
    belongs = (slot_lane == lax.broadcasted_iota(jnp.int32, (slots, edges), 0)).astype(f32)
    spread = dot(ids[...].astype(f32), belongs, (1, 0), HIGHEST)
    where = jnp.sum(jnp.where(mine, spread, 0.0), axis=0, keepdims=True).astype(jnp.int32)
    live = dot(jnp.broadcast_to(counts[...], (8, atoms)).astype(f32), mine.astype(f32), (1, 0), HIGHEST)[0:1, :]
    usable[...] = (slot_lane[0:1, :].astype(f32) < live).astype(f32)
    owned = where < atoms
    ghost = jnp.maximum(where - atoms, 0)
    block = ghost // atoms
    offsets = [block // 9 - 1, (block // 3) % 3 - 1, block % 3 - 1]
    at = []
    for axis, offset in enumerate(offsets):
        if wide[axis] == 1:
            at.append(jnp.zeros_like(offset))
        elif wide[axis] == 2:
            at.append(jnp.abs(offset))
        else:
            at.append(jnp.where(offset == 0, 0, jnp.where(offset == 1 - 2 * parities[axis], 1, 2)))
    inside = jnp.where(
        at[1] == 0, at[0],
        jnp.where(at[0] == 0, wide[0] - 1 + at[1], wide[0] + wide[1] - 1 + (at[1] - 1) * (wide[0] - 1) + at[0] - 1),
    )
    stored = at[2] * (wide[0] * wide[1]) + inside
    row_of = jnp.where(owned, where, stored * atoms + ghost % atoms)
    row_index = lax.broadcasted_iota(jnp.int32, contrast.shape, 0)
    centre = lax.broadcasted_iota(jnp.int32, contrast.shape, 1) % atoms
    chosen = (row_index == row_of).astype(f32)
    picks[...] = chosen.astype(jnp.bfloat16)
    contrast[...] = (chosen - (row_index == centre).astype(f32)).astype(jnp.bfloat16)
    kinds = (lax.broadcasted_iota(jnp.int32, (energy_table.shape[0], atoms), 0) == species[...]).astype(f32)
    coeff[...] = dot(kinds, energy_table[...], (0, 0), HIGHEST)
    slot = lax.broadcasted_iota(jnp.int32, (atoms, atoms), 1)
    target = lax.broadcasted_iota(jnp.int32, (atoms, atoms), 0)
    land = ((target == bound_rows[...]) & (slot < bound_count[...])).astype(f32)
    lands[...] = jnp.concatenate([land, land, land], axis=1)
    shift = [jnp.where(owned, 0, offset).astype(f32) * EDGE for offset in offsets]
    displace[...] = jnp.concatenate(shift + [jnp.zeros((5, edges), f32)], axis=0)


def sigmoid(x):
    return 1.0 / (1.0 + jnp.exp(-x))


def core_kernel(
    geometry,
    picks_in, contrast_in, displace, usable, coeff, places, scalars, vectors, first, second, third,
    gains, *rest,
):
    atoms, slots, channels, blocks, sinks, order = geometry
    tables = len(blocks)
    ghosts = rest[:tables]
    energies, own_out = rest[tables : tables + 2]
    grads = rest[tables + 2 : tables + 2 + len(sinks)]
    table, weights, far, steer, messages, place_rows, dfar, dweights, dsteer = rest[tables + 2 + len(sinks) :]
    halves = channels // LANES
    chunks = 4 * halves
    edges = atoms * slots
    packet = (chunks + 1) * atoms
    scale = slots ** (-0.5)
    readout = channels ** (-0.25)
    rows = sum(blocks) * atoms
    f32, bf16 = jnp.float32, jnp.bfloat16

    def pieces(chunk, own):
        parts = []
        for which, ref in enumerate(ghosts):
            for block in range(blocks[which]):
                if which == 0 and block == 0:
                    parts.append(own)
                else:
                    at = block * packet + chunk * atoms
                    parts.append(ref[at : at + atoms, :])
        return jnp.concatenate(parts, axis=0)

    picks, contrast = picks_in[...], contrast_in[...]

    row = 0
    for which, ref in enumerate(ghosts):
        for block in range(blocks[which]):
            at = block * packet + chunks * atoms
            if row:
                place_rows[:, row : row + atoms] = ref[at : at + atoms, 0:atoms]
            else:
                place_rows[0:3, 0:atoms] = places[...]
                place_rows[3:, 0:atoms] = jnp.zeros((atoms - 3, atoms), f32)
            row += atoms
    apart = joined(dot(thirds(place_rows[...]), contrast, (1, 0)), 8) + displace[...]
    distance = jnp.sqrt(jnp.sum(apart * apart, axis=0, keepdims=True) + SOFTENING)
    direction = apart / distance
    centres = FIRST_CENTRE + SPACING * lax.broadcasted_iota(jnp.int32, (first.shape[0], edges), 0).astype(f32)
    off = distance - centres
    gauss = jnp.exp(-SHARPNESS * off * off)
    pre_one = dot(first[...], gauss.astype(bf16), (0, 0))
    sig_one = sigmoid(pre_one)
    hidden_one = (pre_one * sig_one).astype(bf16)
    pre_two = dot(second[...], hidden_one, (0, 0))
    sig_two = sigmoid(pre_two)
    hidden_two = (pre_two * sig_two * usable[...]).astype(bf16)
    weights[...] = dot(hidden_two, third[...], (0, 0)).astype(bf16)
    spread = (
        lax.broadcasted_iota(jnp.int32, (8, 3 * LANES), 1) // LANES
        == lax.broadcasted_iota(jnp.int32, (8, 3 * LANES), 0)
    ).astype(f32).astype(bf16)
    steer[...] = dot(direction.astype(bf16), spread, (0, 0)).astype(bf16)

    for part in range(4):
        for h in range(halves):
            chunk = part * halves + h
            lanes = slice(h * LANES, (h + 1) * LANES)
            own = scalars[:, lanes] if part == 0 else vectors[part - 1, :, lanes]
            table[:, chunk * LANES : (chunk + 1) * LANES] = pieces(chunk, own).astype(bf16)
    far[...] = dot(picks, table[...], (0, 0)).astype(bf16)

    tile = 2 * atoms
    steps = edges // tile
    third_part = jnp.asarray(1.0 / 3.0, bf16)

    def edge_inputs(step, h):
        at = slice(step * tile, (step + 1) * tile)
        s = far[at, h * LANES : (h + 1) * LANES]
        v = [far[at, ((1 + a) * halves + h) * LANES : ((1 + a) * halves + h + 1) * LANES] for a in range(3)]
        u = [steer[at, a * LANES : (a + 1) * LANES] for a in range(3)]
        w = [weights[at, n * channels + h * LANES : n * channels + (h + 1) * LANES] for n in range(6)]
        return at, s, v, u, w

    def cross(a, b):
        return [a[1] * b[2] - a[2] * b[1], a[2] * b[0] - a[0] * b[2], a[0] * b[1] - a[1] * b[0]]

    def inner(a, b):
        return a[0] * b[0] + a[1] * b[1] + a[2] * b[2]

    for step in range(steps):
        for h in range(halves):
            at, s, v, u, w = edge_inputs(step, h)
            q = inner(u, v)
            along = w[2] * s + w[5] * q
            keep = w[3] - w[5] * third_part
            turned = cross([w[4] * x for x in v], u)
            new = [w[0] * s + w[1] * q] + [along * u[a] + keep * v[a] + turned[a] for a in range(3)]
            for part, value in enumerate(new):
                chunk = part * halves + h
                messages[at, chunk * LANES : (chunk + 1) * LANES] = value
    centre = lax.broadcasted_iota(jnp.int32, (atoms, edges), 1) % atoms
    mine = (centre == lax.broadcasted_iota(jnp.int32, (atoms, edges), 0)).astype(f32).astype(bf16)
    summed = dot(mine, messages[...], (1, 0))

    cotangents = []
    terms = []
    for h in range(halves):
        lanes = slice(h * LANES, (h + 1) * LANES)
        sums = [summed[:, (p * halves + h) * LANES : (p * halves + h + 1) * LANES] for p in range(4)]
        s_out = scalars[:, lanes] + scale * sums[0]
        v_out = [vectors[a, :, lanes] + scale * sums[1 + a] for a in range(3)]
        c = coeff[:, lanes]
        g = gains[:, lanes]
        sig = sigmoid(s_out)
        terms.append(c * s_out * sig + g * inner(v_out, v_out))
        cot_s = readout * c * sig * (1.0 + s_out * (1.0 - sig))
        cot_v = [(2.0 * readout) * g * v_out[a] for a in range(3)]
        cotangents.append([cot_s] + cot_v)
    total = sum(terms[1:], terms[0])
    energies[...] = readout * dot(jnp.ones((8, LANES), f32), total, (1, 1), HIGHEST)[0:1, :]

    pulled = [[(scale * jnp.concatenate([x, x], axis=0)).astype(bf16) for x in c] for c in cotangents]
    for step in range(steps):
        for h in range(halves):
            at, s, v, u, w = edge_inputs(step, h)
            cs, *cv = pulled[h]
            q = inner(u, v)
            along = w[2] * s + w[5] * q
            keep = w[3] - w[5] * third_part
            d = inner(cv, u)
            turn = cross(u, cv)
            spin = cross(cv, v)
            both = inner(cv, v)
            dq = cs * w[1] + w[5] * d
            ds = cs * w[0] + w[2] * d
            dv = [dq * u[a] + keep * cv[a] + w[4] * turn[a] for a in range(3)]
            du = [dq * v[a] + along * cv[a] + w[4] * spin[a] for a in range(3)]
            dw = [cs * s, cs * q, s * d, both, inner(u, spin), q * d - both * third_part]
            for part, value in enumerate([ds] + dv):
                chunk = part * halves + h
                dfar[at, chunk * LANES : (chunk + 1) * LANES] = value
            for n in range(6):
                dweights[at, n * channels + h * LANES : n * channels + (h + 1) * LANES] = dw[n]
            for a in range(3):
                dsteer[at, (a * halves + h) * LANES : (a * halves + h + 1) * LANES] = du[a]

    def put(chunk, value):
        for which, ref in enumerate(grads):
            for block in range(sinks[which]):
                row = (which * len(order) + order[block]) * atoms
                piece = value[row : row + atoms, :]
                at = block * packet + chunk * atoms
                if which == 0 and block == 0:
                    piece = piece + cotangents[chunk % halves][chunk // halves]
                    own_out[chunk * atoms : (chunk + 1) * atoms, :] = piece
                    piece = jnp.zeros_like(piece)
                ref[at : at + atoms, :] = piece

    for chunk in range(chunks):
        put(chunk, dot(picks, dfar[:, chunk * LANES : (chunk + 1) * LANES], (1, 0)))

    dhidden_two = dot(third[...], dweights[...], (1, 1))
    dpre_two = dhidden_two * usable[...] * sig_two * (1.0 + pre_two * (1.0 - sig_two))
    dhidden_one = dot(second[...], dpre_two.astype(bf16), (1, 0))
    dpre_one = dhidden_one * sig_one * (1.0 + pre_one * (1.0 - sig_one))
    dgauss = dot(first[...], dpre_one.astype(bf16), (1, 0))
    ddistance = jnp.sum(dgauss * gauss * off, axis=0, keepdims=True) * (-2.0 * SHARPNESS)
    gather = (
        lax.broadcasted_iota(jnp.int32, (8, 3 * channels), 1) // channels
        == lax.broadcasted_iota(jnp.int32, (8, 3 * channels), 0)
    ).astype(f32).astype(bf16)
    ddirection = dot(gather, dsteer[...], (1, 1))
    radial = jnp.sum(ddirection * direction, axis=0, keepdims=True)
    inv = 1.0 / distance
    dapart = ddirection * inv + (ddistance - radial * inv) * direction
    dspots = joined(dot(thirds(dapart), contrast, (1, 1)), 8)

    for which, ref in enumerate(grads):
        for block in range(sinks[which]):
            at = block * packet + chunks * atoms
            row = (which * len(order) + order[block]) * atoms
            piece = dspots[:, row : row + atoms]
            if row == 0:
                own_out[at : at + atoms, :] = jnp.zeros((atoms, LANES), f32)
                own_out[at : at + atoms, 0:atoms] = piece
                piece = jnp.zeros_like(piece)
            ref[at : at + atoms, :] = jnp.zeros((atoms, LANES), f32)
            ref[at : at + atoms, 0:atoms] = piece


def finish_kernel(energies_in, own, lands, *rest):
    parts = rest[:-8]
    energies, forces, grad_scalars, grad_vectors, moved, scalar_rows, vector_rows, sems = rest[-8:]
    atoms, channels = scalar_rows.shape
    halves = channels // LANES
    chunks = 4 * halves
    copies = [
        pltpu.make_async_copy(a, b, sems.at[n])
        for n, (a, b) in enumerate([
            (energies_in, energies), (moved, forces), (scalar_rows, grad_scalars), (vector_rows, grad_vectors),
        ])
    ]
    copies[0].start()
    value = parts[0][...]
    for ref in parts[1:]:
        value = value + ref[...]
    ghost = [value[c * atoms : (c + 1) * atoms, :] for c in range(chunks + 1)]
    land = lands[...].astype(jnp.bfloat16)
    sums = dot(land, thirds(jnp.concatenate(ghost[:chunks], axis=1)), (1, 0))
    for part in (1, 2, 3, 0):
        for h in range(halves):
            chunk = part * halves + h
            total = own[chunk * atoms : (chunk + 1) * atoms, :] + sums[:, chunk * LANES : (chunk + 1) * LANES]
            lanes = slice(h * LANES, (h + 1) * LANES)
            if part:
                vector_rows[part - 1, :, lanes] = total
            else:
                scalar_rows[:, lanes] = total
        if part == 3:
            copies[3].start()
    copies[2].start()
    spots = joined(dot(thirds(ghost[chunks][:, 0:atoms]), land[:, 0:atoms], (1, 1)), atoms)
    moved[...] = -(own[chunks * atoms :, 0:atoms] + spots)[0:3, :]
    copies[1].start()
    for copy in copies:
        copy.wait()


VMEM = pl.BlockSpec(memory_space=pltpu.VMEM)
SMEM = pl.BlockSpec(memory_space=pltpu.SMEM)


def shards(
    places, scalars, vectors, species, bound_rows, bound_count, neighbour_ids, neighbour_count,
    radial_first, radial_second, radial_third, energy_table, vector_gains,
):
    f32 = jnp.float32
    atoms, channels = scalars.shape
    places, vectors = places.T, vectors.transpose(1, 0, 2)
    boundary = bound_rows.shape[0]
    assert boundary == atoms == 8
    slots = neighbour_ids.shape[0]
    edges = slots * atoms
    halves = channels // LANES
    chunks = 4 * halves
    packet_rows = (chunks + 1) * boundary

    packet = pl.pallas_call(
        pack_kernel,
        out_shape=jax.ShapeDtypeStruct((packet_rows, LANES), f32),
        in_specs=[SMEM] + [pl.BlockSpec(memory_space=pltpu.HBM)] * 4,
        out_specs=VMEM,
        scratch_shapes=[
            pltpu.SMEM(bound_rows.shape, jnp.int32),
            pltpu.VMEM(places.shape, f32),
            pltpu.VMEM(scalars.shape, f32),
            pltpu.VMEM(vectors.shape, f32),
            pltpu.SemaphoreType.DMA((4,)),
        ],
        compiler_params=pltpu.CompilerParams(vmem_limit_bytes=2 << 20),
        name="pack",
    )(bound_count, *[pltpu.with_memory_space_constraint(x, pltpu.HBM) for x in (bound_rows, places, scalars, vectors)])

    perms = {axis: sides(lax.axis_size(axis)) for axis in AXES}
    wide = {axis: 1 + len(perms[axis]) for axis in AXES}
    per_plane = wide["gx"] * wide["gy"]
    rows = per_plane * wide["gz"] * atoms
    beside_x = [lax.ppermute(packet, "gx", pairs) for pairs in perms["gx"]]
    beside_y = [lax.ppermute(packet, "gy", pairs) for pairs in perms["gy"]]
    across = jnp.concatenate(beside_x, axis=0)
    across, ids, counts = lax.optimization_barrier((across, neighbour_ids.T, neighbour_count.reshape(1, atoms)))
    plain = [
        places, scalars, vectors, radial_first, radial_second, radial_third, vector_gains.reshape(1, channels),
    ]
    parities = jnp.stack([lax.axis_index(a) % 2 if lax.axis_size(a) % 2 == 0 else 0 for a in AXES])
    prepared = pl.pallas_call(
        functools.partial(prep_kernel, tuple(wide[a] for a in AXES)),
        out_shape=[
            jax.ShapeDtypeStruct((rows, edges), jnp.bfloat16),
            jax.ShapeDtypeStruct((rows, edges), jnp.bfloat16),
            jax.ShapeDtypeStruct((8, edges), f32),
            jax.ShapeDtypeStruct((1, edges), f32),
            jax.ShapeDtypeStruct((atoms, channels), f32),
            jax.ShapeDtypeStruct((atoms, 3 * atoms), f32),
        ]
        + [jax.ShapeDtypeStruct(x.shape, x.dtype) for x in plain],
        in_specs=[SMEM] + [VMEM] * (6 + len(plain)),
        out_specs=[VMEM] * (6 + len(plain)),
        compiler_params=pltpu.CompilerParams(vmem_limit_bytes=2 << 20),
        name="prep",
    )(
        parities, ids, counts, species.reshape(1, atoms), energy_table,
        bound_rows.reshape(1, boundary), bound_count.reshape(1, 1), *plain,
    )
    prepared, plain = prepared[:6], prepared[6:]
    *prepared, lands = prepared
    corners = [lax.ppermute(across, "gy", pairs) for pairs in perms["gy"]]
    cross = jnp.concatenate([packet, across] + beside_y, axis=0)
    corner = jnp.concatenate(corners, axis=0)
    tables = [packet, across] + beside_y + corners
    for pairs in perms["gz"]:
        tables += [lax.ppermute(cross, "gz", pairs), lax.ppermute(corner, "gz", pairs)]
    blocks = tuple(t.shape[0] // packet_rows for t in tables)
    sinks = (per_plane,) * wide["gz"]

    nx, ny = wide["gx"], wide["gy"]
    order = [x for x in range(nx)]
    for y in range(1, ny):
        order += [nx + y - 1] + [nx + ny - 1 + (y - 1) * (nx - 1) + x - 1 for x in range(1, nx)]
    geometry = (atoms, slots, channels, blocks, sinks, tuple(order))
    out = pl.pallas_call(
        functools.partial(core_kernel, geometry),
        out_shape=[
            jax.ShapeDtypeStruct((1, atoms), f32),
            jax.ShapeDtypeStruct(((chunks + 1) * atoms, LANES), f32),
        ]
        + [jax.ShapeDtypeStruct((n * packet_rows, LANES), f32) for n in sinks],
        in_specs=[VMEM] * (12 + len(tables)),
        out_specs=[VMEM] * (2 + len(sinks)),
        scratch_shapes=[
            pltpu.VMEM((rows, chunks * LANES), jnp.bfloat16),
            pltpu.VMEM((edges, 6 * channels), jnp.bfloat16),
            pltpu.VMEM((edges, chunks * LANES), jnp.bfloat16),
            pltpu.VMEM((edges, 3 * LANES), jnp.bfloat16),
            pltpu.VMEM((edges, chunks * LANES), jnp.bfloat16),
            pltpu.VMEM((atoms, rows), f32),
            pltpu.VMEM((edges, chunks * LANES), jnp.bfloat16),
            pltpu.VMEM((edges, 6 * channels), jnp.bfloat16),
            pltpu.VMEM((edges, 3 * channels), jnp.bfloat16),
        ],
        compiler_params=pltpu.CompilerParams(vmem_limit_bytes=16 << 20),
        name="edges",
    )(
        *prepared, *plain, *tables,
    )
    energies, own, *grads = out

    plane = grads[0]
    for n, pairs in enumerate(perms["gz"]):
        plane = plane + lax.ppermute(grads[n + 1], "gz", inverse(pairs))
    step = wide["gx"] * packet_rows
    line = plane[:step]
    for n, pairs in backwards(perms["gy"]):
        line = line + lax.ppermute(plane[(n + 1) * step : (n + 2) * step], "gy", inverse(pairs))
    parts = [line[:packet_rows]]
    for n, pairs in backwards(perms["gx"]):
        parts.append(lax.ppermute(line[(n + 1) * packet_rows : (n + 2) * packet_rows], "gx", inverse(pairs)))

    energies, forces, grad_scalars, grad_vectors = pl.pallas_call(
        finish_kernel,
        out_shape=[
            jax.ShapeDtypeStruct((1, atoms), f32),
            jax.ShapeDtypeStruct((3, atoms), f32),
            jax.ShapeDtypeStruct((atoms, channels), f32),
            jax.ShapeDtypeStruct((3, atoms, channels), f32),
        ],
        in_specs=[VMEM] * (3 + len(parts)),
        out_specs=[pl.BlockSpec(memory_space=pltpu.HBM)] * 4,
        scratch_shapes=[
            pltpu.VMEM((3, atoms), f32),
            pltpu.VMEM((atoms, channels), f32),
            pltpu.VMEM((3, atoms, channels), f32),
            pltpu.SemaphoreType.DMA((4,)),
        ],
        compiler_params=pltpu.CompilerParams(vmem_limit_bytes=2 << 20),
        name="finish",
    )(energies, own, lands, *parts)
    return energies.reshape(atoms), forces.T, grad_scalars, grad_vectors.transpose(1, 0, 2)


def solution(mesh):
    every = AXES
    in_specs = (
        P(every, None), P(every, None), P(every, None, None), P(every), P(every), P(every),
        P(None, every), P(every), P(), P(), P(), P(), P(),
    )
    out_specs = (P(every), P(every, None), P(every, None), P(every, None, None))

    return jax.shard_map(shards, mesh=mesh, in_specs=in_specs, out_specs=out_specs, check_vma=False)
```

profile of v0, /device:TPU:0, one launch (start us, length us, event | category | flops | bytes accessed | tf_op | source)
XLA Modules:
  0.0 39.9 jit_solution(7736985229461592976)
XLA Ops:
  1.3 1.0 %pack.1.rest_0_ = f32[72,128]{1,0:T(8,128)S(1)} custom-call(s32[1]{0:T(128)} %copy.17.bound_count, s32[8]{0:T(128)} %bound_rows_in.1, f32[3,8]{1,0:T(4,128)} %bitcast.17, f32[8,256]{1,0:T(8,128)} %rest_1_.1, f32[3,8,256]{2,1,0:T(8,128)} %bitcast.15), custom_call_target="tpu_custom_call" | custom-call | tf_op jit(solution)/shard_map/pack/pallas_call | solution.py:389
  2.3 5.1 %collective-permute-start.1 = (f32[72,128]{1,0:T(8,128)S(1)}, f32[72,128]{1,0:T(8,128)S(1)}, u32[]{:S(2)}, u32[]{:S(2)}) collective-permute-start(f32[72,128]{1,0:T(8,128)S(1)} %pack.1.rest_0_), channel_id=1, source_target_pairs={{8,16},{24,0},{16,8},{0,24},{9,17},{25,1},{17,9},{1,25},{10,18},{2... | collective-permute-start | bytes 110600 | tf_op jit(solution)/shard_map/ppermute | solution.py:409
  7.4 0.0 collective-permute-start
  7.4 2.4 %collective-permute-start.3 = (f32[72,128]{1,0:T(8,128)S(1)}, f32[72,128]{1,0:T(8,128)S(1)}, u32[]{:S(2)}, u32[]{:S(2)}) collective-permute-start(f32[72,128]{1,0:T(8,128)S(1)} %pack.1.rest_0_), channel_id=1, source_target_pairs={{2,4},{6,0},{4,2},{0,6},{3,5},{7,1},{5,3},{1,7},{10,12},{14,8},{12... | collective-permute-start | bytes 110600 | tf_op jit(solution)/shard_map/ppermute | solution.py:410
  9.9 0.5 %collective-permute-start.2 = (f32[72,128]{1,0:T(8,128)S(1)}, f32[72,128]{1,0:T(8,128)S(1)}, u32[]{:S(2)}, u32[]{:S(2)}) collective-permute-start(f32[72,128]{1,0:T(8,128)S(1)} %pack.1.rest_0_), channel_id=1, source_target_pairs={{0,2},{4,6},{2,0},{6,4},{1,3},{5,7},{3,1},{7,5},{8,10},{12,14},{10... | collective-permute-start | bytes 110600 | tf_op jit(solution)/shard_map/ppermute | solution.py:410
  10.4 0.0 collective-permute-done.1
  10.4 1.0 %collective-permute-done = f32[72,128]{1,0:T(8,128)S(1)} collective-permute-done((f32[72,128]{1,0:T(8,128)S(1)}, f32[72,128]{1,0:T(8,128)S(1)}, u32[]{:S(2)}, u32[]{:S(2)}) %collective-permute-start) | collective-permute-done | bytes 36896 | tf_op jit(solution)/shard_map/ppermute | solution.py:409
  11.4 2.4 %collective-permute-start.5 = (f32[144,128]{1,0:T(8,128)S(1)}, f32[144,128]{1,0:T(8,128)S(1)}, u32[]{:S(2)}, u32[]{:S(2)}) collective-permute-start(f32[144,128]{1,0:T(8,128)S(1)} %pad_maximum_fusion.2.rest_1_), channel_id=1, source_target_pairs={{2,4},{6,0},{4,2},{0,6},{3,5},{7,1},{5,3},{1,7},{10,12},{14,8},{12... | collective-permute-start | bytes 221192 | tf_op jit(solution)/shard_map/ppermute | solution.py:438
  13.8 0.5 %collective-permute-start.4 = (f32[144,128]{1,0:T(8,128)S(1)}, f32[144,128]{1,0:T(8,128)S(1)}, u32[]{:S(2)}, u32[]{:S(2)}) collective-permute-start(f32[144,128]{1,0:T(8,128)S(1)} %pad_maximum_fusion.2.rest_1_), channel_id=1, source_target_pairs={{0,2},{4,6},{2,0},{6,4},{1,3},{5,7},{3,1},{7,5},{8,10},{12,14},{10... | collective-permute-start | bytes 221192 | tf_op jit(solution)/shard_map/ppermute | solution.py:438
  14.3 0.0 collective-permute-done.3.rest_3_
  14.4 0.0 collective-permute-done.2.rest_2_
  14.4 0.0 copy-start
  14.4 0.1 collective-permute-start.6
  14.5 2.2 %collective-permute-done.5.rest_5_ = f32[144,128]{1,0:T(8,128)S(1)} collective-permute-done((f32[144,128]{1,0:T(8,128)S(1)}, f32[144,128]{1,0:T(8,128)S(1)}, u32[]{:S(2)}, u32[]{:S(2)}) %collective-permute-start.5) | collective-permute-done | bytes 73760 | tf_op jit(solution)/shard_map/ppermute | solution.py:438
  16.6 1.5 %collective-permute-done.4.rest_4_ = f32[144,128]{1,0:T(8,128)S(1)} collective-permute-done((f32[144,128]{1,0:T(8,128)S(1)}, f32[144,128]{1,0:T(8,128)S(1)}, u32[]{:S(2)}, u32[]{:S(2)}) %collective-permute-start.4) | collective-permute-done | bytes 73760 | tf_op jit(solution)/shard_map/ppermute | solution.py:438
  18.2 0.1 collective-permute-start.7
  18.3 0.0 copy-start.9
  18.3 0.0 copy-start.11
  18.3 0.0 copy-start.4
  18.3 0.0 copy-start.7
  18.3 0.0 copy-start.5
  18.3 0.0 copy-start.6
  18.3 0.0 copy-start.3
  18.4 0.0 copy-start.1
  18.4 0.0 copy-start.2
  18.4 0.1 pad_add_fusion.parities
  18.5 0.5 %copy-done.9 = f32[256]{0:T(256)S(1)} copy-done((f32[256]{0:T(256)S(1)}, f32[256]{0:T(256)}, u32[]{:S(2)}) %copy-start.9) | copy-done | bytes 1048
  19.0 0.0 copy-done.4
  19.0 0.0 copy-done.7
  19.0 0.0 copy-done.5
  19.0 0.0 copy-done.6
  19.0 0.0 copy-done.3
  19.1 0.0 copy-done.1
  19.1 0.0 copy-done.8
  19.1 0.0 copy-done.10
  19.1 0.8 %prep.1 = (bf16[144,128]{1,0:T(8,128)(2,1)S(1)}, bf16[144,128]{1,0:T(8,128)(2,1)S(1)}, f32[8,128]{1,0:T(8,128)S(1)}, f32[1,128]{1,0:T(1,128)S(1)}, f32[8,256]{1,...) custom-call(s32[3]{0:T(128)S(1)} %pad_add_fusion.parities, ...), custom_call_target="tpu_custom_call" | custom-call | tf_op jit(solution)/shard_map/prep/pallas_call | solution.py:417
  19.9 2.6 %edges.1 = (f32[1,8]{1,0:T(1,128)S(1)}, f32[72,128]{1,0:T(8,128)S(1)}, f32[648,128]{1,0:T(8,128)S(1)}, f32[648,128]{1,0:T(8,128)S(1)}) custom-call(bf16[144,128]{1,0:T(8,128)(2,1)S(1)} %get-tuple-element.30.picks_in, bf16[144,128]{1,0:T(8,128)(2,1)S(1)} %get-tuple-element.31.contrast_in, f32[8,128]{1,0:T(8,128)S(1)} %get-tuple-element.32.displace, ...), custom_call_target="tpu_custom_call" | custom-call | tf_op jit(solution)/shard_map/edges/pallas_call | solution.py:452
  22.6 0.5 %collective-permute-start.8 = (f32[648,128]{1,0:T(8,128)S(1)}, f32[648,128]{1,0:T(8,128)S(1)}, u32[]{:S(2)}, u32[]{:S(2)}) collective-permute-start(f32[648,128]{1,0:T(8,128)S(1)} %get-tuple-element.47), channel_id=1, source_target_pairs={{1,0},{0,1},{3,2},{2,3},{5,4},{4,5},{7,6},{6,7},{9,8},{8,9},{11,10... | collective-permute-start | bytes 995336 | tf_op jit(solution)/shard_map/ppermute | solution.py:481
  23.1 1.3 %collective-permute-done.8 = f32[648,128]{1,0:T(8,128)S(1)} collective-permute-done((f32[648,128]{1,0:T(8,128)S(1)}, f32[648,128]{1,0:T(8,128)S(1)}, u32[]{:S(2)}, u32[]{:S(2)}) %collective-permute-start.8) | collective-permute-done | bytes 331808 | tf_op jit(solution)/shard_map/ppermute | solution.py:481
  24.4 1.0 %collective-permute-start.9 = (f32[216,128]{1,0:T(8,128)S(1)}, f32[216,128]{1,0:T(8,128)S(1)}, u32[]{:S(2)}, u32[]{:S(2)}) collective-permute-start(f32[216,128]{1,0:T(8,128)S(1)} %get-tuple-element.52), channel_id=1, source_target_pairs={{4,2},{0,6},{2,4},{6,0},{5,3},{1,7},{3,5},{7,1},{12,10},{8,14},{10... | collective-permute-start | bytes 331784 | tf_op jit(solution)/shard_map/ppermute | solution.py:485
  25.4 1.1 %collective-permute-start.10 = (f32[216,128]{1,0:T(8,128)S(1)}, f32[216,128]{1,0:T(8,128)S(1)}, u32[]{:S(2)}, u32[]{:S(2)}) collective-permute-start(f32[216,128]{1,0:T(8,128)S(1)} %get-tuple-element.53), channel_id=1, source_target_pairs={{2,0},{6,4},{0,2},{4,6},{3,1},{7,5},{1,3},{5,7},{10,8},{14,12},{8,... | collective-permute-start | bytes 331784 | tf_op jit(solution)/shard_map/ppermute | solution.py:485
  26.5 4.9 %collective-permute-done.9 = f32[216,128]{1,0:T(8,128)S(1)} collective-permute-done((f32[216,128]{1,0:T(8,128)S(1)}, f32[216,128]{1,0:T(8,128)S(1)}, u32[]{:S(2)}, u32[]{:S(2)}) %collective-permute-start.9) | collective-permute-done | bytes 110624 | tf_op jit(solution)/shard_map/ppermute | solution.py:485
  31.3 0.8 %collective-permute-done.10 = f32[216,128]{1,0:T(8,128)S(1)} collective-permute-done((f32[216,128]{1,0:T(8,128)S(1)}, f32[216,128]{1,0:T(8,128)S(1)}, u32[]{:S(2)}, u32[]{:S(2)}) %collective-permute-start.10) | collective-permute-done | bytes 110624 | tf_op jit(solution)/shard_map/ppermute | solution.py:485
  32.2 1.2 %collective-permute-start.12 = (f32[72,128]{1,0:T(8,128)S(1)}, f32[72,128]{1,0:T(8,128)S(1)}, u32[]{:S(2)}, u32[]{:S(2)}) collective-permute-start(f32[72,128]{1,0:T(8,128)S(1)} %get-tuple-element.54), channel_id=1, source_target_pairs={{8,0},{24,16},{0,8},{16,24},{9,1},{25,17},{1,9},{17,25},{10,2},{26... | collective-permute-start | bytes 110600 | tf_op jit(solution)/shard_map/ppermute | solution.py:488
  33.4 0.8 %collective-permute-start.11 = (f32[72,128]{1,0:T(8,128)S(1)}, f32[72,128]{1,0:T(8,128)S(1)}, u32[]{:S(2)}, u32[]{:S(2)}) collective-permute-start(f32[72,128]{1,0:T(8,128)S(1)} %get-tuple-element.55), channel_id=1, source_target_pairs={{16,8},{0,24},{8,16},{24,0},{17,9},{1,25},{9,17},{25,1},{18,10},{2... | collective-permute-start | bytes 110600 | tf_op jit(solution)/shard_map/ppermute | solution.py:488
  34.2 2.0 %collective-permute-done.12.rest_2_ = f32[72,128]{1,0:T(8,128)S(1)} collective-permute-done((f32[72,128]{1,0:T(8,128)S(1)}, f32[72,128]{1,0:T(8,128)S(1)}, u32[]{:S(2)}, u32[]{:S(2)}) %collective-permute-start.12) | collective-permute-done | bytes 36896 | tf_op jit(solution)/shard_map/ppermute | solution.py:488
  36.2 2.9 %collective-permute-done.11.rest_1_ = f32[72,128]{1,0:T(8,128)S(1)} collective-permute-done((f32[72,128]{1,0:T(8,128)S(1)}, f32[72,128]{1,0:T(8,128)S(1)}, u32[]{:S(2)}, u32[]{:S(2)}) %collective-permute-start.11) | collective-permute-done | bytes 36896 | tf_op jit(solution)/shard_map/ppermute | solution.py:488
  39.1 0.8 %finish.1 = (f32[1,8]{1,0:T(1,128)}, f32[3,8]{1,0:T(4,128)}, f32[8,256]{1,0:T(8,128)}, f32[3,8,256]{2,1,0:T(8,128)}) custom-call(f32[1,8]{1,0:T(1,128)S(1)} %get-tuple-element.43.energies_in, f32[72,128]{1,0:T(8,128)S(1)} %get-tuple-element.44.own, f32[8,24]{1,0:T(8,128)S(1)} %get-tuple-element.45.lands, f32[72,128]{1,0:T(8,128)S(1)} %get-tuple-element.56.rest_0_, ...), custom_call_target="tpu_custom_call" | custom-call | tf_op jit(solution)/shard_map/finish/pallas_call | solution.py:490
  (14 shorter events, 0.1 us)
Async XLA Ops:
  2.3 8.1 %collective-permute-start.1 = (f32[72,128]{1,0:T(8,128)S(1)}, f32[72,128]{1,0:T(8,128)S(1)}, u32[]{:S(2)}, u32[]{:S(2)}) collective-permute-start(f32[72,128]{1,0:T(8,128)S(1)} %pack.1.rest_0_), channel_id=1, source_target_pairs={{8,16},{24,0},{16,8},{0,24},{9,17},{25,1},{17,9},{1,25},{10,18},{2... | collective-permute-start | bytes 110600 | tf_op jit(solution)/shard_map/ppermute | solution.py:409
  7.4 4.0 %collective-permute-start = (f32[72,128]{1,0:T(8,128)S(1)}, f32[72,128]{1,0:T(8,128)S(1)}, u32[]{:S(2)}, u32[]{:S(2)}) collective-permute-start(f32[72,128]{1,0:T(8,128)S(1)} %pack.1.rest_0_), channel_id=1, source_target_pairs={{0,8},{16,24},{8,0},{24,16},{1,9},{17,25},{9,1},{25,17},{2,10},{18... | collective-permute-start | bytes 110600 | tf_op jit(solution)/shard_map/ppermute | solution.py:409
  7.4 6.9 %collective-permute-start.3 = (f32[72,128]{1,0:T(8,128)S(1)}, f32[72,128]{1,0:T(8,128)S(1)}, u32[]{:S(2)}, u32[]{:S(2)}) collective-permute-start(f32[72,128]{1,0:T(8,128)S(1)} %pack.1.rest_0_), channel_id=1, source_target_pairs={{2,4},{6,0},{4,2},{0,6},{3,5},{7,1},{5,3},{1,7},{10,12},{14,8},{12... | collective-permute-start | bytes 110600 | tf_op jit(solution)/shard_map/ppermute | solution.py:410
  9.9 4.5 %collective-permute-start.2 = (f32[72,128]{1,0:T(8,128)S(1)}, f32[72,128]{1,0:T(8,128)S(1)}, u32[]{:S(2)}, u32[]{:S(2)}) collective-permute-start(f32[72,128]{1,0:T(8,128)S(1)} %pack.1.rest_0_), channel_id=1, source_target_pairs={{0,2},{4,6},{2,0},{6,4},{1,3},{5,7},{3,1},{7,5},{8,10},{12,14},{10... | collective-permute-start | bytes 110600 | tf_op jit(solution)/shard_map/ppermute | solution.py:410
  11.4 5.3 %collective-permute-start.5 = (f32[144,128]{1,0:T(8,128)S(1)}, f32[144,128]{1,0:T(8,128)S(1)}, u32[]{:S(2)}, u32[]{:S(2)}) collective-permute-start(f32[144,128]{1,0:T(8,128)S(1)} %pad_maximum_fusion.2.rest_1_), channel_id=1, source_target_pairs={{2,4},{6,0},{4,2},{0,6},{3,5},{7,1},{5,3},{1,7},{10,12},{14,8},{12... | collective-permute-start | bytes 221192 | tf_op jit(solution)/shard_map/ppermute | solution.py:438
  13.8 4.4 %collective-permute-start.4 = (f32[144,128]{1,0:T(8,128)S(1)}, f32[144,128]{1,0:T(8,128)S(1)}, u32[]{:S(2)}, u32[]{:S(2)}) collective-permute-start(f32[144,128]{1,0:T(8,128)S(1)} %pad_maximum_fusion.2.rest_1_), channel_id=1, source_target_pairs={{0,2},{4,6},{2,0},{6,4},{1,3},{5,7},{3,1},{7,5},{8,10},{12,14},{10... | collective-permute-start | bytes 221192 | tf_op jit(solution)/shard_map/ppermute | solution.py:438
  14.4 4.1 %copy-start = (bf16[64,1536]{1,0:T(8,128)(2,1)S(1)}, bf16[64,1536]{1,0:T(8,128)(2,1)}, u32[]{:S(2)}) copy-start(bf16[64,1536]{1,0:T(8,128)(2,1)} %rest_5_.1) | copy-start | bytes 589828
  14.4 5.5 %collective-permute-start.6 = (f32[360,128]{1,0:T(8,128)S(1)}, f32[360,128]{1,0:T(8,128)S(1)}, u32[]{:S(2)}, u32[]{:S(2)}) collective-permute-start(f32[360,128]{1,0:T(8,128)S(1)} %pad_maximum_fusion), channel_id=1, source_target_pairs={{0,1},{1,0},{2,3},{3,2},{4,5},{5,4},{6,7},{7,6},{8,9},{9,8},{10,11... | collective-permute-start | bytes 552968 | tf_op jit(solution)/shard_map/ppermute | solution.py:443
  18.2 1.7 %collective-permute-start.7 = (f32[288,128]{1,0:T(8,128)S(1)}, f32[288,128]{1,0:T(8,128)S(1)}, u32[]{:S(2)}, u32[]{:S(2)}) collective-permute-start(f32[288,128]{1,0:T(8,128)S(1)} %pad_maximum_fusion.1), channel_id=1, source_target_pairs={{0,1},{1,0},{2,3},{3,2},{4,5},{5,4},{6,7},{7,6},{8,9},{9,8},{10,11... | collective-permute-start | bytes 442376 | tf_op jit(solution)/shard_map/ppermute | solution.py:443
  18.3 0.7 %copy-start.9 = (f32[256]{0:T(256)S(1)}, f32[256]{0:T(256)}, u32[]{:S(2)}) copy-start(f32[256]{0:T(256)} %param.25) | copy-start | bytes 3076
  18.3 0.7 %copy-start.11 = (s32[8]{0:T(128)S(1)}, s32[8]{0:T(128)}, u32[]{:S(2)}) copy-start(s32[8]{0:T(128)} %param.16) | copy-start | bytes 100
  18.3 0.7 %copy-start.4 = (f32[8,3]{0,1:T(4,128)S(1)}, f32[8,3]{0,1:T(4,128)}, u32[]{:S(2)}) copy-start(f32[8,3]{0,1:T(4,128)} %param.13) | copy-start | bytes 292
  18.3 0.7 %copy-start.7 = (bf16[8,64]{1,0:T(8,128)(2,1)S(1)}, bf16[8,64]{1,0:T(8,128)(2,1)}, u32[]{:S(2)}) copy-start(bf16[8,64]{1,0:T(8,128)(2,1)} %rest_3_.1) | copy-start | bytes 3076
  18.3 0.7 %copy-start.5 = (s32[16,8]{0,1:T(8,128)S(1)}, s32[16,8]{0,1:T(8,128)}, u32[]{:S(2)}) copy-start(s32[16,8]{0,1:T(8,128)} %param.19) | copy-start | bytes 1540
  18.3 0.7 %copy-start.6 = (f32[4,256]{1,0:T(4,128)S(1)}, f32[4,256]{1,0:T(4,128)}, u32[]{:S(2)}) copy-start(f32[4,256]{1,0:T(4,128)} %energy_table.1) | copy-start | bytes 12292
  18.3 0.7 %copy-start.3 = (bf16[64,64]{1,0:T(8,128)(2,1)S(1)}, bf16[64,64]{1,0:T(8,128)(2,1)}, u32[]{:S(2)}) copy-start(bf16[64,64]{1,0:T(8,128)(2,1)} %rest_4_.1) | copy-start | bytes 24580
  18.4 0.8 %copy-start.1 = (f32[8,3,256]{2,0,1:T(8,128)S(1)}, f32[8,3,256]{2,0,1:T(8,128)}, u32[]{:S(2)}) copy-start(f32[8,3,256]{2,0,1:T(8,128)} %param.15) | copy-start | bytes 73732
  18.4 0.7 %copy-start.2 = (f32[8,256]{1,0:T(8,128)S(1)}, f32[8,256]{1,0:T(8,128)}, u32[]{:S(2)}) copy-start(f32[8,256]{1,0:T(8,128)} %rest_1_.1) | copy-start | bytes 24580
  18.5 0.7 %copy-start.8 = (s32[8]{0:T(128)S(1)}, s32[8]{0:T(128)}, u32[]{:S(2)}) copy-start(s32[8]{0:T(128)} %bound_rows_in.1) | copy-start | bytes 100
  18.5 0.7 %copy-start.10 = (s32[8]{0:T(128)S(1)}, s32[8]{0:T(128)}, u32[]{:S(2)}) copy-start(s32[8]{0:T(128)} %param.20) | copy-start | bytes 100
  22.6 1.8 %collective-permute-start.8 = (f32[648,128]{1,0:T(8,128)S(1)}, f32[648,128]{1,0:T(8,128)S(1)}, u32[]{:S(2)}, u32[]{:S(2)}) collective-permute-start(f32[648,128]{1,0:T(8,128)S(1)} %get-tuple-element.47), channel_id=1, source_target_pairs={{1,0},{0,1},{3,2},{2,3},{5,4},{4,5},{7,6},{6,7},{9,8},{8,9},{11,10... | collective-permute-start | bytes 995336 | tf_op jit(solution)/shard_map/ppermute | solution.py:481
  24.4 6.9 %collective-permute-start.9 = (f32[216,128]{1,0:T(8,128)S(1)}, f32[216,128]{1,0:T(8,128)S(1)}, u32[]{:S(2)}, u32[]{:S(2)}) collective-permute-start(f32[216,128]{1,0:T(8,128)S(1)} %get-tuple-element.52), channel_id=1, source_target_pairs={{4,2},{0,6},{2,4},{6,0},{5,3},{1,7},{3,5},{7,1},{12,10},{8,14},{10... | collective-permute-start | bytes 331784 | tf_op jit(solution)/shard_map/ppermute | solution.py:485
  25.4 6.7 %collective-permute-start.10 = (f32[216,128]{1,0:T(8,128)S(1)}, f32[216,128]{1,0:T(8,128)S(1)}, u32[]{:S(2)}, u32[]{:S(2)}) collective-permute-start(f32[216,128]{1,0:T(8,128)S(1)} %get-tuple-element.53), channel_id=1, source_target_pairs={{2,0},{6,4},{0,2},{4,6},{3,1},{7,5},{1,3},{5,7},{10,8},{14,12},{8,... | collective-permute-start | bytes 331784 | tf_op jit(solution)/shard_map/ppermute | solution.py:485
  32.2 4.0 %collective-permute-start.12 = (f32[72,128]{1,0:T(8,128)S(1)}, f32[72,128]{1,0:T(8,128)S(1)}, u32[]{:S(2)}, u32[]{:S(2)}) collective-permute-start(f32[72,128]{1,0:T(8,128)S(1)} %get-tuple-element.54), channel_id=1, source_target_pairs={{8,0},{24,16},{0,8},{16,24},{9,1},{25,17},{1,9},{17,25},{10,2},{26... | collective-permute-start | bytes 110600 | tf_op jit(solution)/shard_map/ppermute | solution.py:488
  33.4 5.8 %collective-permute-start.11 = (f32[72,128]{1,0:T(8,128)S(1)}, f32[72,128]{1,0:T(8,128)S(1)}, u32[]{:S(2)}, u32[]{:S(2)}) collective-permute-start(f32[72,128]{1,0:T(8,128)S(1)} %get-tuple-element.55), channel_id=1, source_target_pairs={{16,8},{0,24},{8,16},{24,0},{17,9},{1,25},{9,17},{25,1},{18,10},{2... | collective-permute-start | bytes 110600 | tf_op jit(solution)/shard_map/ppermute | solution.py:488
where the time goes:
time: 40.2 us; the launch traced here: 39.9 us
  waiting for transfers between devices  16.6 us (41%)
  starting transfers between devices  15.8 us (39%)
  Pallas kernels  5.13 us (13%)
  between operations  1.48 us (4%)
  local copies, waits for them, and re-layouts  0.74 us (2%)
    ppermute x2, waiting for transfers between devices, shards(): lax.ppermute(plane[(n + 1) * step:(n + 2) * step], 'gy', inverse(pairs))  5.68 us
    ppermute x2, starting transfers between devices, shards(): beside_x = [lax.ppermute(packet, 'gx', pairs) for pairs in perms['gx']]  5.15 us
    ppermute x2, waiting for transfers between devices, shards(): lax.ppermute(line[(n + 1) * packet_rows:(n + 2) * packet_rows], 'gx', inv...  4.93 us
    ppermute x2, waiting for transfers between devices, shards(): corners = [lax.ppermute(across, 'gy', pairs) for pairs in perms['gy']]  3.7 us
    ppermute x2, starting transfers between devices, shards(): beside_y = [lax.ppermute(packet, 'gy', pairs) for pairs in perms['gy']]  2.98 us
    ppermute x2, starting transfers between devices, shards(): corners = [lax.ppermute(across, 'gy', pairs) for pairs in perms['gy']]  2.98 us
    pallas_call x1, Pallas kernels, shards(): pl.pallas_call(functools.partial(core_kernel, geometry), out_shape=[jax.S...  2.62 us
    ppermute x2, starting transfers between devices, shards(): lax.ppermute(plane[(n + 1) * step:(n + 2) * step], 'gy', inverse(pairs))  2.04 us
  transfers between devices with their start and end apart: 13, of which 8 were waited for; matrix products, arithmetic and copies ran while one was open for 0% of the time, Pallas kernels for 2%

commit v1 on v0

--- a/solution.py
+++ b/solution.py
@@ -145,12 +145,12 @@
     picks_in, contrast_in, displace, usable, coeff, places, scalars, vectors, first, second, third,
     gains, *rest,
 ):
-    atoms, slots, channels, blocks, sinks, order = geometry
+    atoms, slots, channels, blocks, sinks = geometry
     tables = len(blocks)
     ghosts = rest[:tables]
     energies, own_out = rest[tables : tables + 2]
     grads = rest[tables + 2 : tables + 2 + len(sinks)]
-    table, weights, far, steer, messages, place_rows, dfar, dweights, dsteer = rest[tables + 2 + len(sinks) :]
+    table, weights, far, steer, place_rows = rest[tables + 2 + len(sinks) :]
     halves = channels // LANES
     chunks = 4 * halves
     edges = atoms * slots
@@ -195,12 +195,12 @@
     pre_two = dot(second[...], hidden_one, (0, 0))
     sig_two = sigmoid(pre_two)
     hidden_two = (pre_two * sig_two * usable[...]).astype(bf16)
-    weights[...] = dot(hidden_two, third[...], (0, 0)).astype(bf16)
+    weights[...] = dot(hidden_two, third[...], (0, 0))
     spread = (
         lax.broadcasted_iota(jnp.int32, (8, 3 * LANES), 1) // LANES
         == lax.broadcasted_iota(jnp.int32, (8, 3 * LANES), 0)
     ).astype(f32).astype(bf16)
-    steer[...] = dot(direction.astype(bf16), spread, (0, 0)).astype(bf16)
+    steer[...] = dot(direction.astype(bf16), spread, (0, 0))
 
     for part in range(4):
         for h in range(halves):
@@ -208,7 +208,7 @@
             lanes = slice(h * LANES, (h + 1) * LANES)
             own = scalars[:, lanes] if part == 0 else vectors[part - 1, :, lanes]
             table[:, chunk * LANES : (chunk + 1) * LANES] = pieces(chunk, own).astype(bf16)
-    far[...] = dot(picks, table[...], (0, 0)).astype(bf16)
+    far[...] = dot(picks, table[...], (0, 0))
 
     tile = 2 * atoms
     steps = edges // tile
@@ -216,10 +216,10 @@
 
     def edge_inputs(step, h):
         at = slice(step * tile, (step + 1) * tile)
-        s = far[at, h * LANES : (h + 1) * LANES]
-        v = [far[at, ((1 + a) * halves + h) * LANES : ((1 + a) * halves + h + 1) * LANES] for a in range(3)]
-        u = [steer[at, a * LANES : (a + 1) * LANES] for a in range(3)]
-        w = [weights[at, n * channels + h * LANES : n * channels + (h + 1) * LANES] for n in range(6)]
+        s = far[at, h * LANES : (h + 1) * LANES].astype(bf16)
+        v = [far[at, ((1 + a) * halves + h) * LANES : ((1 + a) * halves + h + 1) * LANES].astype(bf16) for a in range(3)]
+        u = [steer[at, a * LANES : (a + 1) * LANES].astype(bf16) for a in range(3)]
+        w = [weights[at, n * channels + h * LANES : n * channels + (h + 1) * LANES].astype(bf16) for n in range(6)]
         return at, s, v, u, w
 
     def cross(a, b):
@@ -228,6 +228,10 @@
     def inner(a, b):
         return a[0] * b[0] + a[1] * b[1] + a[2] * b[2]
 
+    def stacked(values, first, last):
+        return jnp.concatenate([jnp.concatenate(values[n], axis=0) for n in range(first, last)], axis=1)
+
+    messages = [[] for _ in range(chunks)]
     for step in range(steps):
         for h in range(halves):
             at, s, v, u, w = edge_inputs(step, h)
@@ -237,11 +241,10 @@
             turned = cross([w[4] * x for x in v], u)
             new = [w[0] * s + w[1] * q] + [along * u[a] + keep * v[a] + turned[a] for a in range(3)]
             for part, value in enumerate(new):
-                chunk = part * halves + h
-                messages[at, chunk * LANES : (chunk + 1) * LANES] = value
+                messages[part * halves + h].append(value)
     centre = lax.broadcasted_iota(jnp.int32, (atoms, edges), 1) % atoms
     mine = (centre == lax.broadcasted_iota(jnp.int32, (atoms, edges), 0)).astype(f32).astype(bf16)
-    summed = dot(mine, messages[...], (1, 0))
+    summed = dot(mine, stacked(messages, 0, chunks), (1, 0))
 
     cotangents = []
     terms = []
@@ -260,6 +263,7 @@
     total = sum(terms[1:], terms[0])
     energies[...] = readout * dot(jnp.ones((8, LANES), f32), total, (1, 1), HIGHEST)[0:1, :]
 
+    dfar, dweights, dsteer = [[[] for _ in range(n * halves)] for n in (4, 6, 3)]
     pulled = [[(scale * jnp.concatenate([x, x], axis=0)).astype(bf16) for x in c] for c in cotangents]
     for step in range(steps):
         for h in range(halves):
@@ -278,29 +282,27 @@
             du = [dq * v[a] + along * cv[a] + w[4] * spin[a] for a in range(3)]
             dw = [cs * s, cs * q, s * d, both, inner(u, spin), q * d - both * third_part]
             for part, value in enumerate([ds] + dv):
-                chunk = part * halves + h
-                dfar[at, chunk * LANES : (chunk + 1) * LANES] = value
+                dfar[part * halves + h].append(value)
             for n in range(6):
-                dweights[at, n * channels + h * LANES : n * channels + (h + 1) * LANES] = dw[n]
+                dweights[n * halves + h].append(dw[n])
             for a in range(3):
-                dsteer[at, (a * halves + h) * LANES : (a * halves + h + 1) * LANES] = du[a]
+                dsteer[a * halves + h].append(du[a])
 
     def put(chunk, value):
-        for which, ref in enumerate(grads):
-            for block in range(sinks[which]):
-                row = (which * len(order) + order[block]) * atoms
-                piece = value[row : row + atoms, :]
-                at = block * packet + chunk * atoms
-                if which == 0 and block == 0:
+        for members, ref in zip(sinks, grads):
+            for n, block in enumerate(members):
+                piece = value[block * atoms : (block + 1) * atoms, :]
+                at = n * packet + chunk * atoms
+                if block == 0:
                     piece = piece + cotangents[chunk % halves][chunk // halves]
                     own_out[chunk * atoms : (chunk + 1) * atoms, :] = piece
                     piece = jnp.zeros_like(piece)
                 ref[at : at + atoms, :] = piece
 
     for chunk in range(chunks):
-        put(chunk, dot(picks, dfar[:, chunk * LANES : (chunk + 1) * LANES], (1, 0)))
-
-    dhidden_two = dot(third[...], dweights[...], (1, 1))
+        put(chunk, dot(picks, stacked(dfar, chunk, chunk + 1), (1, 0)))
+
+    dhidden_two = dot(third[...], stacked(dweights, 0, 6 * halves), (1, 1))
     dpre_two = dhidden_two * usable[...] * sig_two * (1.0 + pre_two * (1.0 - sig_two))
     dhidden_one = dot(second[...], dpre_two.astype(bf16), (1, 0))
     dpre_one = dhidden_one * sig_one * (1.0 + pre_one * (1.0 - sig_one))
@@ -310,20 +312,19 @@
         lax.broadcasted_iota(jnp.int32, (8, 3 * channels), 1) // channels
         == lax.broadcasted_iota(jnp.int32, (8, 3 * channels), 0)
     ).astype(f32).astype(bf16)
-    ddirection = dot(gather, dsteer[...], (1, 1))
+    ddirection = dot(gather, stacked(dsteer, 0, 3 * halves), (1, 1))
     radial = jnp.sum(ddirection * direction, axis=0, keepdims=True)
     inv = 1.0 / distance
     dapart = ddirection * inv + (ddistance - radial * inv) * direction
     dspots = joined(dot(thirds(dapart), contrast, (1, 1)), 8)
 
-    for which, ref in enumerate(grads):
-        for block in range(sinks[which]):
-            at = block * packet + chunks * atoms
-            row = (which * len(order) + order[block]) * atoms
-            piece = dspots[:, row : row + atoms]
-            if row == 0:
-                own_out[at : at + atoms, :] = jnp.zeros((atoms, LANES), f32)
-                own_out[at : at + atoms, 0:atoms] = piece
+    for members, ref in zip(sinks, grads):
+        for n, block in enumerate(members):
+            at = n * packet + chunks * atoms
+            piece = dspots[:, block * atoms : (block + 1) * atoms]
+            if block == 0:
+                own_out[chunks * atoms :, :] = jnp.zeros((atoms, LANES), f32)
+                own_out[chunks * atoms :, 0:atoms] = piece
                 piece = jnp.zeros_like(piece)
             ref[at : at + atoms, :] = jnp.zeros((atoms, LANES), f32)
             ref[at : at + atoms, 0:atoms] = piece
@@ -437,37 +438,36 @@
     *prepared, lands = prepared
     corners = [lax.ppermute(across, "gy", pairs) for pairs in perms["gy"]]
     cross = jnp.concatenate([packet, across] + beside_y, axis=0)
-    corner = jnp.concatenate(corners, axis=0)
     tables = [packet, across] + beside_y + corners
     for pairs in perms["gz"]:
-        tables += [lax.ppermute(cross, "gz", pairs), lax.ppermute(corner, "gz", pairs)]
+        tables.append(lax.ppermute(cross, "gz", pairs))
+        tables += [lax.ppermute(c, "gz", pairs) for c in corners]
     blocks = tuple(t.shape[0] // packet_rows for t in tables)
-    sinks = (per_plane,) * wide["gz"]
-
     nx, ny = wide["gx"], wide["gy"]
-    order = [x for x in range(nx)]
-    for y in range(1, ny):
-        order += [nx + y - 1] + [nx + ny - 1 + (y - 1) * (nx - 1) + x - 1 for x in range(1, nx)]
-    geometry = (atoms, slots, channels, blocks, sinks, tuple(order))
+    sinks = []
+    for z in range(wide["gz"]):
+        first = z * per_plane
+        sinks.append(tuple(range(first, first + nx)))
+        for y in range(1, ny):
+            corner = first + nx + ny - 1 + (y - 1) * (nx - 1)
+            sinks.append((first + nx + y - 1, *range(corner, corner + nx - 1)))
+
+    geometry = (atoms, slots, channels, blocks, tuple(sinks))
     out = pl.pallas_call(
         functools.partial(core_kernel, geometry),
         out_shape=[
             jax.ShapeDtypeStruct((1, atoms), f32),
             jax.ShapeDtypeStruct(((chunks + 1) * atoms, LANES), f32),
         ]
-        + [jax.ShapeDtypeStruct((n * packet_rows, LANES), f32) for n in sinks],
+        + [jax.ShapeDtypeStruct((len(n) * packet_rows, LANES), f32) for n in sinks],
         in_specs=[VMEM] * (12 + len(tables)),
         out_specs=[VMEM] * (2 + len(sinks)),
         scratch_shapes=[
             pltpu.VMEM((rows, chunks * LANES), jnp.bfloat16),
-            pltpu.VMEM((edges, 6 * channels), jnp.bfloat16),
-            pltpu.VMEM((edges, chunks * LANES), jnp.bfloat16),
-            pltpu.VMEM((edges, 3 * LANES), jnp.bfloat16),
-            pltpu.VMEM((edges, chunks * LANES), jnp.bfloat16),
+            pltpu.VMEM((edges, 6 * channels), f32),
+            pltpu.VMEM((edges, chunks * LANES), f32),
+            pltpu.VMEM((edges, 3 * LANES), f32),
             pltpu.VMEM((atoms, rows), f32),
-            pltpu.VMEM((edges, chunks * LANES), jnp.bfloat16),
-            pltpu.VMEM((edges, 6 * channels), jnp.bfloat16),
-            pltpu.VMEM((edges, 3 * channels), jnp.bfloat16),
         ],
         compiler_params=pltpu.CompilerParams(vmem_limit_bytes=16 << 20),
         name="edges",
@@ -476,13 +476,13 @@
     )
     energies, own, *grads = out
 
-    plane = grads[0]
+    lines = grads[:ny]
     for n, pairs in enumerate(perms["gz"]):
-        plane = plane + lax.ppermute(grads[n + 1], "gz", inverse(pairs))
-    step = wide["gx"] * packet_rows
-    line = plane[:step]
-    for n, pairs in backwards(perms["gy"]):
-        line = line + lax.ppermute(plane[(n + 1) * step : (n + 2) * step], "gy", inverse(pairs))
+        back = [lax.ppermute(grads[(n + 1) * ny + y], "gz", inverse(pairs)) for y in range(ny)]
+        lines = [a + b for a, b in zip(lines, back)]
+    line = lines[0]
+    for n, pairs in enumerate(perms["gy"]):
+        line = line + lax.ppermute(lines[n + 1], "gy", inverse(pairs))
     parts = [line[:packet_rows]]
     for n, pairs in backwards(perms["gx"]):
         parts.append(lax.ppermute(line[(n + 1) * packet_rows : (n + 2) * packet_rows], "gx", inverse(pairs)))

time: 40.2 us -> 39.1 us (0.973)
  waiting for transfers between devices: 16.6 us -> 15.5 us
  starting transfers between devices: 15.8 us -> 16.4 us
  Pallas kernels: 5.13 us -> 4.66 us
    ppermute x5 -> x8, waiting for transfers between devices: 6.95 us -> 6.04 us  [the longest x2 5.58 us: shards(): line = line + lax.ppermute(lines[n + 1], 'gy', inverse(pairs))]
    ppermute x5 -> x8, starting transfers between devices: 2.71 us -> 3.23 us  [the longest x2 2.1 us: shards(): line = line + lax.ppermute(lines[n + 1], 'gy', inverse(pairs))]
    pallas_call x1, Pallas kernels: 2.62 us -> 2.15 us  [shards(): pl.pallas_call(functools.partial(core_kernel, geometry), out_shape=[jax.S...]
  transfers between devices with their start and end apart: 13 -> 16, of which waited for: 8 -> 8; matrix products, arithmetic and copies ran while one was open for 0% -> 0% of each run, Pallas kernels for 2% -> 2%
where the time goes in v1:
time: 39.1 us; the launch traced here: 38.9 us
  starting transfers between devices  16.4 us (42%)
  waiting for transfers between devices  15.5 us (40%)
  Pallas kernels  4.66 us (12%)
  between operations  1.53 us (4%)
  local copies, waits for them, and re-layouts  0.65 us (2%)
    ppermute x2, waiting for transfers between devices, shards(): line = line + lax.ppermute(lines[n + 1], 'gy', inverse(pairs))  5.58 us
    ppermute x2, starting transfers between devices, shards(): beside_x = [lax.ppermute(packet, 'gx', pairs) for pairs in perms['gx']]  5.15 us
    ppermute x2, waiting for transfers between devices, shards(): lax.ppermute(line[(n + 1) * packet_rows:(n + 2) * packet_rows], 'gx', inv...  4.94 us
    ppermute x2, waiting for transfers between devices, shards(): corners = [lax.ppermute(across, 'gy', pairs) for pairs in perms['gy']]  3.58 us
    ppermute x2, starting transfers between devices, shards(): corners = [lax.ppermute(across, 'gy', pairs) for pairs in perms['gy']]  3.05 us
    ppermute x2, starting transfers between devices, shards(): beside_y = [lax.ppermute(packet, 'gy', pairs) for pairs in perms['gy']]  2.98 us
    pallas_call x1, Pallas kernels, shards(): pl.pallas_call(functools.partial(core_kernel, geometry), out_shape=[jax.S...  2.15 us
    ppermute x2, starting transfers between devices, shards(): line = line + lax.ppermute(lines[n + 1], 'gy', inverse(pairs))  2.1 us
  transfers between devices with their start and end apart: 16, of which 8 were waited for; matrix products, arithmetic and copies ran while one was open for 0% of the time, Pallas kernels for 2%

profile of v1, /device:TPU:0, one launch (start us, length us, event | category | flops | bytes accessed | tf_op | source)
XLA Modules:
  0.0 38.9 jit_solution(17032189092509092730)
XLA Ops:
  1.3 1.0 %pack.1.rest_0_ = f32[72,128]{1,0:T(8,128)S(1)} custom-call(s32[1]{0:T(128)} %copy.17.bound_count, s32[8]{0:T(128)} %bound_rows_in.1, f32[3,8]{1,0:T(4,128)} %bitcast.17, f32[8,256]{1,0:T(8,128)} %rest_1_.1, f32[3,8,256]{2,1,0:T(8,128)} %bitcast.15), custom_call_target="tpu_custom_call" | custom-call | tf_op jit(solution)/shard_map/pack/pallas_call | solution.py:390
  2.3 5.1 %collective-permute-start.1 = (f32[72,128]{1,0:T(8,128)S(1)}, f32[72,128]{1,0:T(8,128)S(1)}, u32[]{:S(2)}, u32[]{:S(2)}) collective-permute-start(f32[72,128]{1,0:T(8,128)S(1)} %pack.1.rest_0_), channel_id=1, source_target_pairs={{8,16},{24,0},{16,8},{0,24},{9,17},{25,1},{17,9},{1,25},{10,18},{2... | collective-permute-start | bytes 110600 | tf_op jit(solution)/shard_map/ppermute | solution.py:410
  7.4 0.0 collective-permute-start
  7.4 2.4 %collective-permute-start.3 = (f32[72,128]{1,0:T(8,128)S(1)}, f32[72,128]{1,0:T(8,128)S(1)}, u32[]{:S(2)}, u32[]{:S(2)}) collective-permute-start(f32[72,128]{1,0:T(8,128)S(1)} %pack.1.rest_0_), channel_id=1, source_target_pairs={{2,4},{6,0},{4,2},{0,6},{3,5},{7,1},{5,3},{1,7},{10,12},{14,8},{12... | collective-permute-start | bytes 110600 | tf_op jit(solution)/shard_map/ppermute | solution.py:411
  9.9 0.5 %collective-permute-start.2 = (f32[72,128]{1,0:T(8,128)S(1)}, f32[72,128]{1,0:T(8,128)S(1)}, u32[]{:S(2)}, u32[]{:S(2)}) collective-permute-start(f32[72,128]{1,0:T(8,128)S(1)} %pack.1.rest_0_), channel_id=1, source_target_pairs={{0,2},{4,6},{2,0},{6,4},{1,3},{5,7},{3,1},{7,5},{8,10},{12,14},{10... | collective-permute-start | bytes 110600 | tf_op jit(solution)/shard_map/ppermute | solution.py:411
  10.4 0.0 collective-permute-done.1
  10.4 1.0 %collective-permute-done = f32[72,128]{1,0:T(8,128)S(1)} collective-permute-done((f32[72,128]{1,0:T(8,128)S(1)}, f32[72,128]{1,0:T(8,128)S(1)}, u32[]{:S(2)}, u32[]{:S(2)}) %collective-permute-start) | collective-permute-done | bytes 36896 | tf_op jit(solution)/shard_map/ppermute | solution.py:410
  11.4 2.5 %collective-permute-start.5 = (f32[144,128]{1,0:T(8,128)S(1)}, f32[144,128]{1,0:T(8,128)S(1)}, u32[]{:S(2)}, u32[]{:S(2)}) collective-permute-start(f32[144,128]{1,0:T(8,128)S(1)} %pad_maximum_fusion.1.rest_1_), channel_id=1, source_target_pairs={{2,4},{6,0},{4,2},{0,6},{3,5},{7,1},{5,3},{1,7},{10,12},{14,8},{12... | collective-permute-start | bytes 221192 | tf_op jit(solution)/shard_map/ppermute | solution.py:439
  13.9 0.5 %collective-permute-start.4 = (f32[144,128]{1,0:T(8,128)S(1)}, f32[144,128]{1,0:T(8,128)S(1)}, u32[]{:S(2)}, u32[]{:S(2)}) collective-permute-start(f32[144,128]{1,0:T(8,128)S(1)} %pad_maximum_fusion.1.rest_1_), channel_id=1, source_target_pairs={{0,2},{4,6},{2,0},{6,4},{1,3},{5,7},{3,1},{7,5},{8,10},{12,14},{10... | collective-permute-start | bytes 221192 | tf_op jit(solution)/shard_map/ppermute | solution.py:439
  14.4 0.0 collective-permute-done.3.rest_3_
  14.4 0.0 collective-permute-done.2.rest_2_
  14.4 0.1 collective-permute-start.6
  14.5 0.0 copy-start.7
  14.5 0.0 copy-start.9
  14.6 0.0 copy-start.11
  14.6 0.0 copy-start.5
  14.6 0.0 copy-start.6
  14.6 0.0 copy-start.4
  14.6 0.0 copy-start.3
  14.6 0.0 copy-start.1
  14.6 0.0 copy-start.2
  14.7 2.0 %collective-permute-done.5.rest_5_ = f32[144,128]{1,0:T(8,128)S(1)} collective-permute-done((f32[144,128]{1,0:T(8,128)S(1)}, f32[144,128]{1,0:T(8,128)S(1)}, u32[]{:S(2)}, u32[]{:S(2)}) %collective-permute-start.5) | collective-permute-done | bytes 73760 | tf_op jit(solution)/shard_map/ppermute | solution.py:439
  16.7 0.0 collective-permute-start.8
  16.7 1.5 %collective-permute-done.4.rest_4_ = f32[144,128]{1,0:T(8,128)S(1)} collective-permute-done((f32[144,128]{1,0:T(8,128)S(1)}, f32[144,128]{1,0:T(8,128)S(1)}, u32[]{:S(2)}, u32[]{:S(2)}) %collective-permute-start.4) | collective-permute-done | bytes 73760 | tf_op jit(solution)/shard_map/ppermute | solution.py:439
  18.2 0.0 collective-permute-start.7
  18.2 0.1 pad_add_fusion.parities
  18.4 0.6 %copy-done.8 = s32[8]{0:T(128)S(1)} copy-done((s32[8]{0:T(128)S(1)}, s32[8]{0:T(128)}, u32[]{:S(2)}) %copy-start.8) | copy-done | bytes 56
  19.0 0.0 copy-done.10
  19.0 0.8 %prep.1 = (bf16[144,128]{1,0:T(8,128)(2,1)S(1)}, bf16[144,128]{1,0:T(8,128)(2,1)S(1)}, f32[8,128]{1,0:T(8,128)S(1)}, f32[1,128]{1,0:T(1,128)S(1)}, f32[8,256]{1,...) custom-call(s32[3]{0:T(128)S(1)} %pad_add_fusion.parities, ...), custom_call_target="tpu_custom_call" | custom-call | tf_op jit(solution)/shard_map/prep/pallas_call | solution.py:418
  19.8 0.0 collective-permute-done.8.rest_8_
  19.8 0.0 collective-permute-done.7.rest_7_
  19.8 0.0 collective-permute-done.6.rest_6_
  19.8 2.1 %edges.1 = (f32[1,8]{1,0:T(1,128)S(1)}, f32[72,128]{1,0:T(8,128)S(1)}, f32[216,128]{1,0:T(8,128)S(1)}, f32[216,128]{1,0:T(8,128)S(1)}, f32[216,128]{1,0:T(8,128)...) custom-call(bf16[144,128]{1,0:T(8,128)(2,1)S(1)} %get-tuple-element.34.picks_in, ...), custom_call_target="tpu_custom_call" | custom-call | tf_op jit(solution)/shard_map/edges/pallas_call | solution.py:456
  21.9 0.5 %collective-permute-start.10 = (f32[216,128]{1,0:T(8,128)S(1)}, f32[216,128]{1,0:T(8,128)S(1)}, u32[]{:S(2)}, u32[]{:S(2)}) collective-permute-start(f32[216,128]{1,0:T(8,128)S(1)} %get-tuple-element.53), channel_id=1, source_target_pairs={{1,0},{0,1},{3,2},{2,3},{5,4},{4,5},{7,6},{6,7},{9,8},{8,9},{11,10... | collective-permute-start | bytes 331784 | tf_op jit(solution)/shard_map/ppermute | solution.py:481
  22.5 0.1 collective-permute-start.12
  22.6 0.4 %collective-permute-start.9 = (f32[216,128]{1,0:T(8,128)S(1)}, f32[216,128]{1,0:T(8,128)S(1)}, u32[]{:S(2)}, u32[]{:S(2)}) collective-permute-start(f32[216,128]{1,0:T(8,128)S(1)} %get-tuple-element.51), channel_id=1, source_target_pairs={{1,0},{0,1},{3,2},{2,3},{5,4},{4,5},{7,6},{6,7},{9,8},{8,9},{11,10... | collective-permute-start | bytes 331784 | tf_op jit(solution)/shard_map/ppermute | solution.py:481
  23.0 0.4 %collective-permute-done.10 = f32[216,128]{1,0:T(8,128)S(1)} collective-permute-done((f32[216,128]{1,0:T(8,128)S(1)}, f32[216,128]{1,0:T(8,128)S(1)}, u32[]{:S(2)}, u32[]{:S(2)}) %collective-permute-start.10) | collective-permute-done | bytes 110624 | tf_op jit(solution)/shard_map/ppermute | solution.py:481
  23.5 0.9 %collective-permute-start.11 = (f32[216,128]{1,0:T(8,128)S(1)}, f32[216,128]{1,0:T(8,128)S(1)}, u32[]{:S(2)}, u32[]{:S(2)}) collective-permute-start(f32[216,128]{1,0:T(8,128)S(1)} %add.29), channel_id=1, source_target_pairs={{2,0},{6,4},{0,2},{4,6},{3,1},{7,5},{1,3},{5,7},{10,8},{14,12},{8,... | collective-permute-start | bytes 331784 | tf_op jit(solution)/shard_map/ppermute | solution.py:485
  24.3 0.0 collective-permute-done.12
  24.3 1.2 %collective-permute-start.13 = (f32[216,128]{1,0:T(8,128)S(1)}, f32[216,128]{1,0:T(8,128)S(1)}, u32[]{:S(2)}, u32[]{:S(2)}) collective-permute-start(f32[216,128]{1,0:T(8,128)S(1)} %add.31), channel_id=1, source_target_pairs={{4,2},{0,6},{2,4},{6,0},{5,3},{1,7},{3,5},{7,1},{12,10},{8,14},{10... | collective-permute-start | bytes 331784 | tf_op jit(solution)/shard_map/ppermute | solution.py:485
  25.6 0.0 collective-permute-done.9
  25.6 3.9 %collective-permute-done.11 = f32[216,128]{1,0:T(8,128)S(1)} collective-permute-done((f32[216,128]{1,0:T(8,128)S(1)}, f32[216,128]{1,0:T(8,128)S(1)}, u32[]{:S(2)}, u32[]{:S(2)}) %collective-permute-start.11) | collective-permute-done | bytes 110624 | tf_op jit(solution)/shard_map/ppermute | solution.py:485
  29.5 1.7 %collective-permute-done.13 = f32[216,128]{1,0:T(8,128)S(1)} collective-permute-done((f32[216,128]{1,0:T(8,128)S(1)}, f32[216,128]{1,0:T(8,128)S(1)}, u32[]{:S(2)}, u32[]{:S(2)}) %collective-permute-start.13) | collective-permute-done | bytes 110624 | tf_op jit(solution)/shard_map/ppermute | solution.py:485
  31.2 1.1 %collective-permute-start.15 = (f32[72,128]{1,0:T(8,128)S(1)}, f32[72,128]{1,0:T(8,128)S(1)}, u32[]{:S(2)}, u32[]{:S(2)}) collective-permute-start(f32[72,128]{1,0:T(8,128)S(1)} %get-tuple-element.60), channel_id=1, source_target_pairs={{8,0},{24,16},{0,8},{16,24},{9,1},{25,17},{1,9},{17,25},{10,2},{26... | collective-permute-start | bytes 110600 | tf_op jit(solution)/shard_map/ppermute | solution.py:488
  32.4 0.8 %collective-permute-start.14 = (f32[72,128]{1,0:T(8,128)S(1)}, f32[72,128]{1,0:T(8,128)S(1)}, u32[]{:S(2)}, u32[]{:S(2)}) collective-permute-start(f32[72,128]{1,0:T(8,128)S(1)} %get-tuple-element.61), channel_id=1, source_target_pairs={{16,8},{0,24},{8,16},{24,0},{17,9},{1,25},{9,17},{25,1},{18,10},{2... | collective-permute-start | bytes 110600 | tf_op jit(solution)/shard_map/ppermute | solution.py:488
  33.2 2.1 %collective-permute-done.15.rest_2_ = f32[72,128]{1,0:T(8,128)S(1)} collective-permute-done((f32[72,128]{1,0:T(8,128)S(1)}, f32[72,128]{1,0:T(8,128)S(1)}, u32[]{:S(2)}, u32[]{:S(2)}) %collective-permute-start.15) | collective-permute-done | bytes 36896 | tf_op jit(solution)/shard_map/ppermute | solution.py:488
  35.2 2.9 %collective-permute-done.14.rest_1_ = f32[72,128]{1,0:T(8,128)S(1)} collective-permute-done((f32[72,128]{1,0:T(8,128)S(1)}, f32[72,128]{1,0:T(8,128)S(1)}, u32[]{:S(2)}, u32[]{:S(2)}) %collective-permute-start.14) | collective-permute-done | bytes 36896 | tf_op jit(solution)/shard_map/ppermute | solution.py:488
  38.1 0.8 %finish.1 = (f32[1,8]{1,0:T(1,128)}, f32[3,8]{1,0:T(4,128)}, f32[8,256]{1,0:T(8,128)}, f32[3,8,256]{2,1,0:T(8,128)}) custom-call(f32[1,8]{1,0:T(1,128)S(1)} %get-tuple-element.47.energies_in, f32[72,128]{1,0:T(8,128)S(1)} %get-tuple-element.48.own, f32[8,24]{1,0:T(8,128)S(1)} %get-tuple-element.49.lands, f32[72,128]{1,0:T(8,128)S(1)} %get-tuple-element.62.rest_0_, ...), custom_call_target="tpu_custom_call" | custom-call | tf_op jit(solution)/shard_map/finish/pallas_call | solution.py:490
  (19 shorter events, 0.1 us)
Async XLA Ops:
  2.3 8.1 %collective-permute-start.1 = (f32[72,128]{1,0:T(8,128)S(1)}, f32[72,128]{1,0:T(8,128)S(1)}, u32[]{:S(2)}, u32[]{:S(2)}) collective-permute-start(f32[72,128]{1,0:T(8,128)S(1)} %pack.1.rest_0_), channel_id=1, source_target_pairs={{8,16},{24,0},{16,8},{0,24},{9,17},{25,1},{17,9},{1,25},{10,18},{2... | collective-permute-start | bytes 110600 | tf_op jit(solution)/shard_map/ppermute | solution.py:410
  7.4 4.0 %collective-permute-start = (f32[72,128]{1,0:T(8,128)S(1)}, f32[72,128]{1,0:T(8,128)S(1)}, u32[]{:S(2)}, u32[]{:S(2)}) collective-permute-start(f32[72,128]{1,0:T(8,128)S(1)} %pack.1.rest_0_), channel_id=1, source_target_pairs={{0,8},{16,24},{8,0},{24,16},{1,9},{17,25},{9,1},{25,17},{2,10},{18... | collective-permute-start | bytes 110600 | tf_op jit(solution)/shard_map/ppermute | solution.py:410
  7.4 7.0 %collective-permute-start.3 = (f32[72,128]{1,0:T(8,128)S(1)}, f32[72,128]{1,0:T(8,128)S(1)}, u32[]{:S(2)}, u32[]{:S(2)}) collective-permute-start(f32[72,128]{1,0:T(8,128)S(1)} %pack.1.rest_0_), channel_id=1, source_target_pairs={{2,4},{6,0},{4,2},{0,6},{3,5},{7,1},{5,3},{1,7},{10,12},{14,8},{12... | collective-permute-start | bytes 110600 | tf_op jit(solution)/shard_map/ppermute | solution.py:411
  9.9 4.6 %collective-permute-start.2 = (f32[72,128]{1,0:T(8,128)S(1)}, f32[72,128]{1,0:T(8,128)S(1)}, u32[]{:S(2)}, u32[]{:S(2)}) collective-permute-start(f32[72,128]{1,0:T(8,128)S(1)} %pack.1.rest_0_), channel_id=1, source_target_pairs={{0,2},{4,6},{2,0},{6,4},{1,3},{5,7},{3,1},{7,5},{8,10},{12,14},{10... | collective-permute-start | bytes 110600 | tf_op jit(solution)/shard_map/ppermute | solution.py:411
  11.4 7.0 %copy-start = (bf16[64,1536]{1,0:T(8,128)(2,1)S(1)}, bf16[64,1536]{1,0:T(8,128)(2,1)}, u32[]{:S(2)}) copy-start(bf16[64,1536]{1,0:T(8,128)(2,1)} %rest_5_.1) | copy-start | bytes 589828
  11.4 5.3 %collective-permute-start.5 = (f32[144,128]{1,0:T(8,128)S(1)}, f32[144,128]{1,0:T(8,128)S(1)}, u32[]{:S(2)}, u32[]{:S(2)}) collective-permute-start(f32[144,128]{1,0:T(8,128)S(1)} %pad_maximum_fusion.1.rest_1_), channel_id=1, source_target_pairs={{2,4},{6,0},{4,2},{0,6},{3,5},{7,1},{5,3},{1,7},{10,12},{14,8},{12... | collective-permute-start | bytes 221192 | tf_op jit(solution)/shard_map/ppermute | solution.py:439
  13.9 4.4 %collective-permute-start.4 = (f32[144,128]{1,0:T(8,128)S(1)}, f32[144,128]{1,0:T(8,128)S(1)}, u32[]{:S(2)}, u32[]{:S(2)}) collective-permute-start(f32[144,128]{1,0:T(8,128)S(1)} %pad_maximum_fusion.1.rest_1_), channel_id=1, source_target_pairs={{0,2},{4,6},{2,0},{6,4},{1,3},{5,7},{3,1},{7,5},{8,10},{12,14},{10... | collective-permute-start | bytes 221192 | tf_op jit(solution)/shard_map/ppermute | solution.py:439
  14.4 5.3 %collective-permute-start.6 = (f32[360,128]{1,0:T(8,128)S(1)}, f32[360,128]{1,0:T(8,128)S(1)}, u32[]{:S(2)}, u32[]{:S(2)}) collective-permute-start(f32[360,128]{1,0:T(8,128)S(1)} %pad_maximum_fusion), channel_id=1, source_target_pairs={{0,1},{1,0},{2,3},{3,2},{4,5},{5,4},{6,7},{7,6},{8,9},{9,8},{10,11... | collective-permute-start | bytes 552968 | tf_op jit(solution)/shard_map/ppermute | solution.py:443
  14.5 3.8 %copy-start.7 = (bf16[8,64]{1,0:T(8,128)(2,1)S(1)}, bf16[8,64]{1,0:T(8,128)(2,1)}, u32[]{:S(2)}) copy-start(bf16[8,64]{1,0:T(8,128)(2,1)} %rest_3_.1) | copy-start | bytes 3076
  14.5 3.8 %copy-start.9 = (f32[256]{0:T(256)S(1)}, f32[256]{0:T(256)}, u32[]{:S(2)}) copy-start(f32[256]{0:T(256)} %param.25) | copy-start | bytes 3076
  14.6 3.8 %copy-start.11 = (s32[8]{0:T(128)S(1)}, s32[8]{0:T(128)}, u32[]{:S(2)}) copy-start(s32[8]{0:T(128)} %param.16) | copy-start | bytes 100
  14.6 3.8 %copy-start.5 = (s32[16,8]{0,1:T(8,128)S(1)}, s32[16,8]{0,1:T(8,128)}, u32[]{:S(2)}) copy-start(s32[16,8]{0,1:T(8,128)} %param.19) | copy-start | bytes 1540
  14.6 3.8 %copy-start.6 = (f32[4,256]{1,0:T(4,128)S(1)}, f32[4,256]{1,0:T(4,128)}, u32[]{:S(2)}) copy-start(f32[4,256]{1,0:T(4,128)} %energy_table.1) | copy-start | bytes 12292
  14.6 3.8 %copy-start.4 = (f32[8,3]{0,1:T(4,128)S(1)}, f32[8,3]{0,1:T(4,128)}, u32[]{:S(2)}) copy-start(f32[8,3]{0,1:T(4,128)} %param.13) | copy-start | bytes 292
  14.6 3.8 %copy-start.3 = (bf16[64,64]{1,0:T(8,128)(2,1)S(1)}, bf16[64,64]{1,0:T(8,128)(2,1)}, u32[]{:S(2)}) copy-start(bf16[64,64]{1,0:T(8,128)(2,1)} %rest_4_.1) | copy-start | bytes 24580
  14.6 3.8 %copy-start.1 = (f32[8,3,256]{2,0,1:T(8,128)S(1)}, f32[8,3,256]{2,0,1:T(8,128)}, u32[]{:S(2)}) copy-start(f32[8,3,256]{2,0,1:T(8,128)} %param.15) | copy-start | bytes 73732
  14.6 3.8 %copy-start.2 = (f32[8,256]{1,0:T(8,128)S(1)}, f32[8,256]{1,0:T(8,128)}, u32[]{:S(2)}) copy-start(f32[8,256]{1,0:T(8,128)} %rest_1_.1) | copy-start | bytes 24580
  16.7 3.1 %collective-permute-start.8 = (f32[144,128]{1,0:T(8,128)S(1)}, f32[144,128]{1,0:T(8,128)S(1)}, u32[]{:S(2)}, u32[]{:S(2)}) collective-permute-start(f32[144,128]{1,0:T(8,128)S(1)} %collective-permute-done.5.rest_5_), channel_id=1, source_target_pairs={{0,1},{1,0},{2,3},{3,2},{4,5},{5,4},{6,7},{7,6},{8,9},{9,8},{10,11... | collective-permute-start | bytes 221192 | tf_op jit(solution)/shard_map/ppermute | solution.py:444
  18.2 1.5 %collective-permute-start.7 = (f32[144,128]{1,0:T(8,128)S(1)}, f32[144,128]{1,0:T(8,128)S(1)}, u32[]{:S(2)}, u32[]{:S(2)}) collective-permute-start(f32[144,128]{1,0:T(8,128)S(1)} %collective-permute-done.4.rest_4_), channel_id=1, source_target_pairs={{0,1},{1,0},{2,3},{3,2},{4,5},{5,4},{6,7},{7,6},{8,9},{9,8},{10,11... | collective-permute-start | bytes 221192 | tf_op jit(solution)/shard_map/ppermute | solution.py:444
  18.3 0.7 %copy-start.8 = (s32[8]{0:T(128)S(1)}, s32[8]{0:T(128)}, u32[]{:S(2)}) copy-start(s32[8]{0:T(128)} %bound_rows_in.1) | copy-start | bytes 100
  18.3 0.7 %copy-start.10 = (s32[8]{0:T(128)S(1)}, s32[8]{0:T(128)}, u32[]{:S(2)}) copy-start(s32[8]{0:T(128)} %param.20) | copy-start | bytes 100
  21.9 1.5 %collective-permute-start.10 = (f32[216,128]{1,0:T(8,128)S(1)}, f32[216,128]{1,0:T(8,128)S(1)}, u32[]{:S(2)}, u32[]{:S(2)}) collective-permute-start(f32[216,128]{1,0:T(8,128)S(1)} %get-tuple-element.53), channel_id=1, source_target_pairs={{1,0},{0,1},{3,2},{2,3},{5,4},{4,5},{7,6},{6,7},{9,8},{8,9},{11,10... | collective-permute-start | bytes 331784 | tf_op jit(solution)/shard_map/ppermute | solution.py:481
  22.5 1.8 %collective-permute-start.12 = (f32[216,128]{1,0:T(8,128)S(1)}, f32[216,128]{1,0:T(8,128)S(1)}, u32[]{:S(2)}, u32[]{:S(2)}) collective-permute-start(f32[216,128]{1,0:T(8,128)S(1)} %get-tuple-element.55), channel_id=1, source_target_pairs={{1,0},{0,1},{3,2},{2,3},{5,4},{4,5},{7,6},{6,7},{9,8},{8,9},{11,10... | collective-permute-start | bytes 331784 | tf_op jit(solution)/shard_map/ppermute | solution.py:481
  22.6 3.0 %collective-permute-start.9 = (f32[216,128]{1,0:T(8,128)S(1)}, f32[216,128]{1,0:T(8,128)S(1)}, u32[]{:S(2)}, u32[]{:S(2)}) collective-permute-start(f32[216,128]{1,0:T(8,128)S(1)} %get-tuple-element.51), channel_id=1, source_target_pairs={{1,0},{0,1},{3,2},{2,3},{5,4},{4,5},{7,6},{6,7},{9,8},{8,9},{11,10... | collective-permute-start | bytes 331784 | tf_op jit(solution)/shard_map/ppermute | solution.py:481
  23.5 6.0 %collective-permute-start.11 = (f32[216,128]{1,0:T(8,128)S(1)}, f32[216,128]{1,0:T(8,128)S(1)}, u32[]{:S(2)}, u32[]{:S(2)}) collective-permute-start(f32[216,128]{1,0:T(8,128)S(1)} %add.29), channel_id=1, source_target_pairs={{2,0},{6,4},{0,2},{4,6},{3,1},{7,5},{1,3},{5,7},{10,8},{14,12},{8,... | collective-permute-start | bytes 331784 | tf_op jit(solution)/shard_map/ppermute | solution.py:485
  24.3 6.8 %collective-permute-start.13 = (f32[216,128]{1,0:T(8,128)S(1)}, f32[216,128]{1,0:T(8,128)S(1)}, u32[]{:S(2)}, u32[]{:S(2)}) collective-permute-start(f32[216,128]{1,0:T(8,128)S(1)} %add.31), channel_id=1, source_target_pairs={{4,2},{0,6},{2,4},{6,0},{5,3},{1,7},{3,5},{7,1},{12,10},{8,14},{10... | collective-permute-start | bytes 331784 | tf_op jit(solution)/shard_map/ppermute | solution.py:485
  31.2 4.0 %collective-permute-start.15 = (f32[72,128]{1,0:T(8,128)S(1)}, f32[72,128]{1,0:T(8,128)S(1)}, u32[]{:S(2)}, u32[]{:S(2)}) collective-permute-start(f32[72,128]{1,0:T(8,128)S(1)} %get-tuple-element.60), channel_id=1, source_target_pairs={{8,0},{24,16},{0,8},{16,24},{9,1},{25,17},{1,9},{17,25},{10,2},{26... | collective-permute-start | bytes 110600 | tf_op jit(solution)/shard_map/ppermute | solution.py:488
  32.4 5.8 %collective-permute-start.14 = (f32[72,128]{1,0:T(8,128)S(1)}, f32[72,128]{1,0:T(8,128)S(1)}, u32[]{:S(2)}, u32[]{:S(2)}) collective-permute-start(f32[72,128]{1,0:T(8,128)S(1)} %get-tuple-element.61), channel_id=1, source_target_pairs={{16,8},{0,24},{8,16},{24,0},{17,9},{1,25},{9,17},{25,1},{18,10},{2... | collective-permute-start | bytes 110600 | tf_op jit(solution)/shard_map/ppermute | solution.py:488

commit v2 on v1

--- a/solution.py
+++ b/solution.py
@@ -45,10 +45,6 @@
         return [[((i + 1) % size, i) for i in range(size)], [(i, (i + 1) % size) for i in range(size)]]
     pairs = [[(i, (i + 1) % size) for i in range(first, size, 2)] for first in (0, 1)]
     return [half + [(b, a) for a, b in half] for half in pairs]
-
-
-def backwards(pairs_list):
-    return reversed(list(enumerate(pairs_list)))
 
 
 def inverse(pairs):
@@ -157,7 +153,6 @@
     packet = (chunks + 1) * atoms
     scale = slots ** (-0.5)
     readout = channels ** (-0.25)
-    rows = sum(blocks) * atoms
     f32, bf16 = jnp.float32, jnp.bfloat16
 
     def pieces(chunk, own):
@@ -189,13 +184,18 @@
     centres = FIRST_CENTRE + SPACING * lax.broadcasted_iota(jnp.int32, (first.shape[0], edges), 0).astype(f32)
     off = distance - centres
     gauss = jnp.exp(-SHARPNESS * off * off)
-    pre_one = dot(first[...], gauss.astype(bf16), (0, 0))
-    sig_one = sigmoid(pre_one)
-    hidden_one = (pre_one * sig_one).astype(bf16)
-    pre_two = dot(second[...], hidden_one, (0, 0))
-    sig_two = sigmoid(pre_two)
-    hidden_two = (pre_two * sig_two * usable[...]).astype(bf16)
-    weights[...] = dot(hidden_two, third[...], (0, 0))
+    basis = jnp.concatenate([gauss, gauss * off * (-2.0 * SHARPNESS)], axis=1)
+    hidden = dot(first[...], basis.astype(bf16), (0, 0))
+    for layer in (second[...], None):
+        value, slope = hidden[:, 0:edges], hidden[:, edges:]
+        sig = sigmoid(value)
+        value, slope = value * sig, slope * sig * (1.0 + value * (1.0 - sig))
+        if layer is None:
+            value, slope = value * usable[...], slope * usable[...]
+        hidden = jnp.concatenate([value, slope], axis=1).astype(bf16)
+        if layer is not None:
+            hidden = dot(layer, hidden, (0, 0))
+    weights[0:edges, :] = dot(hidden[:, 0:edges], third[...], (0, 0))
     spread = (
         lax.broadcasted_iota(jnp.int32, (8, 3 * LANES), 1) // LANES
         == lax.broadcasted_iota(jnp.int32, (8, 3 * LANES), 0)
@@ -221,6 +221,10 @@
         u = [steer[at, a * LANES : (a + 1) * LANES].astype(bf16) for a in range(3)]
         w = [weights[at, n * channels + h * LANES : n * channels + (h + 1) * LANES].astype(bf16) for n in range(6)]
         return at, s, v, u, w
+
+    def slopes(step, h):
+        at = slice(edges + step * tile, edges + (step + 1) * tile)
+        return [weights[at, n * channels + h * LANES : n * channels + (h + 1) * LANES].astype(bf16) for n in range(6)]
 
     def cross(a, b):
         return [a[1] * b[2] - a[2] * b[1], a[2] * b[0] - a[0] * b[2], a[0] * b[1] - a[1] * b[0]]
@@ -242,6 +246,7 @@
             new = [w[0] * s + w[1] * q] + [along * u[a] + keep * v[a] + turned[a] for a in range(3)]
             for part, value in enumerate(new):
                 messages[part * halves + h].append(value)
+    weights[edges:, :] = dot(hidden[:, edges:], third[...], (0, 0))
     centre = lax.broadcasted_iota(jnp.int32, (atoms, edges), 1) % atoms
     mine = (centre == lax.broadcasted_iota(jnp.int32, (atoms, edges), 0)).astype(f32).astype(bf16)
     summed = dot(mine, stacked(messages, 0, chunks), (1, 0))
@@ -263,7 +268,7 @@
     total = sum(terms[1:], terms[0])
     energies[...] = readout * dot(jnp.ones((8, LANES), f32), total, (1, 1), HIGHEST)[0:1, :]
 
-    dfar, dweights, dsteer = [[[] for _ in range(n * halves)] for n in (4, 6, 3)]
+    dfar, dsteer = [[[] for _ in range(n * halves)] for n in (4, 5)]
     pulled = [[(scale * jnp.concatenate([x, x], axis=0)).astype(bf16) for x in c] for c in cotangents]
     for step in range(steps):
         for h in range(halves):
@@ -275,24 +280,25 @@
             d = inner(cv, u)
             turn = cross(u, cv)
             spin = cross(cv, v)
-            both = inner(cv, v)
             dq = cs * w[1] + w[5] * d
             ds = cs * w[0] + w[2] * d
             dv = [dq * u[a] + keep * cv[a] + w[4] * turn[a] for a in range(3)]
             du = [dq * v[a] + along * cv[a] + w[4] * spin[a] for a in range(3)]
-            dw = [cs * s, cs * q, s * d, both, inner(u, spin), q * d - both * third_part]
+            g = slopes(step, h)
+            stretch = [
+                s * (cs * g[0] + d * g[2]) + q * (cs * g[1] + d * g[5]),
+                inner(cv, v) * (g[3] - g[5] * third_part) + inner(u, spin) * g[4],
+            ]
             for part, value in enumerate([ds] + dv):
                 dfar[part * halves + h].append(value)
-            for n in range(6):
-                dweights[n * halves + h].append(dw[n])
-            for a in range(3):
-                dsteer[a * halves + h].append(du[a])
+            for a, value in enumerate(du + stretch):
+                dsteer[a * halves + h].append(value)
 
     def put(chunk, value):
         for members, ref in zip(sinks, grads):
             for n, block in enumerate(members):
                 piece = value[block * atoms : (block + 1) * atoms, :]
-                at = n * packet + chunk * atoms
+                at = (n * chunks + chunk) * atoms
                 if block == 0:
                     piece = piece + cotangents[chunk % halves][chunk // halves]
                     own_out[chunk * atoms : (chunk + 1) * atoms, :] = piece
@@ -302,32 +308,28 @@
     for chunk in range(chunks):
         put(chunk, dot(picks, stacked(dfar, chunk, chunk + 1), (1, 0)))
 
-    dhidden_two = dot(third[...], stacked(dweights, 0, 6 * halves), (1, 1))
-    dpre_two = dhidden_two * usable[...] * sig_two * (1.0 + pre_two * (1.0 - sig_two))
-    dhidden_one = dot(second[...], dpre_two.astype(bf16), (1, 0))
-    dpre_one = dhidden_one * sig_one * (1.0 + pre_one * (1.0 - sig_one))
-    dgauss = dot(first[...], dpre_one.astype(bf16), (1, 0))
-    ddistance = jnp.sum(dgauss * gauss * off, axis=0, keepdims=True) * (-2.0 * SHARPNESS)
     gather = (
-        lax.broadcasted_iota(jnp.int32, (8, 3 * channels), 1) // channels
-        == lax.broadcasted_iota(jnp.int32, (8, 3 * channels), 0)
+        jnp.minimum(lax.broadcasted_iota(jnp.int32, (8, 5 * channels), 1) // channels, 3)
+        == lax.broadcasted_iota(jnp.int32, (8, 5 * channels), 0)
     ).astype(f32).astype(bf16)
-    ddirection = dot(gather, stacked(dsteer, 0, 3 * halves), (1, 1))
+    ddirection = dot(gather, stacked(dsteer, 0, 5 * halves), (1, 1))
+    ddistance = ddirection[3:4, :]
     radial = jnp.sum(ddirection * direction, axis=0, keepdims=True)
     inv = 1.0 / distance
-    dapart = ddirection * inv + (ddistance - radial * inv) * direction
+    component = lax.broadcasted_iota(jnp.int32, (8, edges), 0) < 3
+    dapart = jnp.where(component, ddirection * inv, 0.0) + (ddistance - radial * inv) * direction
     dspots = joined(dot(thirds(dapart), contrast, (1, 1)), 8)
 
     for members, ref in zip(sinks, grads):
+        at = len(members) * chunks * atoms
+        ref[at:, :] = jnp.zeros((atoms, LANES), f32)
         for n, block in enumerate(members):
-            at = n * packet + chunks * atoms
             piece = dspots[:, block * atoms : (block + 1) * atoms]
             if block == 0:
                 own_out[chunks * atoms :, :] = jnp.zeros((atoms, LANES), f32)
                 own_out[chunks * atoms :, 0:atoms] = piece
-                piece = jnp.zeros_like(piece)
-            ref[at : at + atoms, :] = jnp.zeros((atoms, LANES), f32)
-            ref[at : at + atoms, 0:atoms] = piece
+            else:
+                ref[at:, n * atoms : (n + 1) * atoms] = piece
 
 
 def finish_kernel(energies_in, own, lands, *rest):
@@ -343,12 +345,13 @@
         ])
     ]
     copies[0].start()
-    value = parts[0][...]
-    for ref in parts[1:]:
-        value = value + ref[...]
-    ghost = [value[c * atoms : (c + 1) * atoms, :] for c in range(chunks + 1)]
+    values = [ref[0 : chunks * atoms, :] for ref in parts]
+    value = sum(values[1:], values[0])
+    spots = [ref[ref.shape[0] - atoms :, n * atoms : (n + 1) * atoms] for n, ref in enumerate(parts)]
+    spots = sum(spots[1:], spots[0])
+    ghost = [value[c * atoms : (c + 1) * atoms, :] for c in range(chunks)]
     land = lands[...].astype(jnp.bfloat16)
-    sums = dot(land, thirds(jnp.concatenate(ghost[:chunks], axis=1)), (1, 0))
+    sums = dot(land, thirds(jnp.concatenate(ghost, axis=1)), (1, 0))
     for part in (1, 2, 3, 0):
         for h in range(halves):
             chunk = part * halves + h
@@ -361,7 +364,7 @@
         if part == 3:
             copies[3].start()
     copies[2].start()
-    spots = joined(dot(thirds(ghost[chunks][:, 0:atoms]), land[:, 0:atoms], (1, 1)), atoms)
+    spots = joined(dot(thirds(spots), land[:, 0:atoms], (1, 1)), atoms)
     moved[...] = -(own[chunks * atoms :, 0:atoms] + spots)[0:3, :]
     copies[1].start()
     for copy in copies:
@@ -459,12 +462,12 @@
             jax.ShapeDtypeStruct((1, atoms), f32),
             jax.ShapeDtypeStruct(((chunks + 1) * atoms, LANES), f32),
         ]
-        + [jax.ShapeDtypeStruct((len(n) * packet_rows, LANES), f32) for n in sinks],
+        + [jax.ShapeDtypeStruct(((len(n) * chunks + 1) * boundary, LANES), f32) for n in sinks],
         in_specs=[VMEM] * (12 + len(tables)),
         out_specs=[VMEM] * (2 + len(sinks)),
         scratch_shapes=[
             pltpu.VMEM((rows, chunks * LANES), jnp.bfloat16),
-            pltpu.VMEM((edges, 6 * channels), f32),
+            pltpu.VMEM((2 * edges, 6 * channels), f32),
             pltpu.VMEM((edges, chunks * LANES), f32),
             pltpu.VMEM((edges, 3 * LANES), f32),
             pltpu.VMEM((atoms, rows), f32),
@@ -483,9 +486,10 @@
     line = lines[0]
     for n, pairs in enumerate(perms["gy"]):
         line = line + lax.ppermute(lines[n + 1], "gy", inverse(pairs))
-    parts = [line[:packet_rows]]
-    for n, pairs in backwards(perms["gx"]):
-        parts.append(lax.ppermute(line[(n + 1) * packet_rows : (n + 2) * packet_rows], "gx", inverse(pairs)))
+    parts, span = [line], chunks * boundary
+    for n, pairs in enumerate(perms["gx"]):
+        value = jnp.concatenate([line[(n + 1) * span : (n + 2) * span], line[-boundary:]], axis=0)
+        parts.append(lax.ppermute(value, "gx", inverse(pairs)))
 
     energies, forces, grad_scalars, grad_vectors = pl.pallas_call(
         finish_kernel,

time: 39.1 us -> 37.8 us (0.967)
  waiting for transfers between devices: 15.5 us -> 14.6 us
    ppermute x2, waiting for transfers between devices: 4.94 us -> 4.33 us  [shards(): parts.append(lax.ppermute(value, 'gx', inverse(pairs)))]
where the time goes in v2:
time: 37.8 us; the launch traced here: 37.6 us
  starting transfers between devices  16.3 us (43%)
  waiting for transfers between devices  14.6 us (39%)
  Pallas kernels  4.36 us (12%)
  between operations  1.55 us (4%)
  local copies, waits for them, and re-layouts  0.66 us (2%)
    ppermute x2, waiting for transfers between devices, shards(): line = line + lax.ppermute(lines[n + 1], 'gy', inverse(pairs))  5.22 us
    ppermute x2, starting transfers between devices, shards(): beside_x = [lax.ppermute(packet, 'gx', pairs) for pairs in perms['gx']]  5.15 us
    ppermute x2, waiting for transfers between devices, shards(): parts.append(lax.ppermute(value, 'gx', inverse(pairs)))  4.33 us
    ppermute x2, waiting for transfers between devices, shards(): corners = [lax.ppermute(across, 'gy', pairs) for pairs in perms['gy']]  3.58 us
    ppermute x2, starting transfers between devices, shards(): corners = [lax.ppermute(across, 'gy', pairs) for pairs in perms['gy']]  3.05 us
    ppermute x2, starting transfers between devices, shards(): beside_y = [lax.ppermute(packet, 'gy', pairs) for pairs in perms['gy']]  2.98 us
    ppermute x2, starting transfers between devices, shards(): line = line + lax.ppermute(lines[n + 1], 'gy', inverse(pairs))  2.1 us
    ppermute x2, starting transfers between devices, shards(): parts.append(lax.ppermute(value, 'gx', inverse(pairs)))  1.88 us
  transfers between devices with their start and end apart: 16, of which 8 were waited for; matrix products, arithmetic and copies ran while one was open for 0% of the time, Pallas kernels for 2%

profile of v2, /device:TPU:0, one launch (start us, length us, event | category | flops | bytes accessed | tf_op | source)
XLA Modules:
  0.0 37.6 jit_solution(1522652706102045407)
XLA Ops:
  1.3 1.0 %pack.1.rest_0_ = f32[72,128]{1,0:T(8,128)S(1)} custom-call(s32[1]{0:T(128)} %copy.17.bound_count, s32[8]{0:T(128)} %bound_rows_in.1, f32[3,8]{1,0:T(4,128)} %bitcast.17, f32[8,256]{1,0:T(8,128)} %rest_1_.1, f32[3,8,256]{2,1,0:T(8,128)} %bitcast.15), custom_call_target="tpu_custom_call" | custom-call | tf_op jit(solution)/shard_map/pack/pallas_call | solution.py:393
  2.3 5.1 %collective-permute-start.1 = (f32[72,128]{1,0:T(8,128)S(1)}, f32[72,128]{1,0:T(8,128)S(1)}, u32[]{:S(2)}, u32[]{:S(2)}) collective-permute-start(f32[72,128]{1,0:T(8,128)S(1)} %pack.1.rest_0_), channel_id=1, source_target_pairs={{8,16},{24,0},{16,8},{0,24},{9,17},{25,1},{17,9},{1,25},{10,18},{2... | collective-permute-start | bytes 110600 | tf_op jit(solution)/shard_map/ppermute | solution.py:413
  7.4 0.0 collective-permute-start
  7.4 2.4 %collective-permute-start.3 = (f32[72,128]{1,0:T(8,128)S(1)}, f32[72,128]{1,0:T(8,128)S(1)}, u32[]{:S(2)}, u32[]{:S(2)}) collective-permute-start(f32[72,128]{1,0:T(8,128)S(1)} %pack.1.rest_0_), channel_id=1, source_target_pairs={{2,4},{6,0},{4,2},{0,6},{3,5},{7,1},{5,3},{1,7},{10,12},{14,8},{12... | collective-permute-start | bytes 110600 | tf_op jit(solution)/shard_map/ppermute | solution.py:414
  9.9 0.5 %collective-permute-start.2 = (f32[72,128]{1,0:T(8,128)S(1)}, f32[72,128]{1,0:T(8,128)S(1)}, u32[]{:S(2)}, u32[]{:S(2)}) collective-permute-start(f32[72,128]{1,0:T(8,128)S(1)} %pack.1.rest_0_), channel_id=1, source_target_pairs={{0,2},{4,6},{2,0},{6,4},{1,3},{5,7},{3,1},{7,5},{8,10},{12,14},{10... | collective-permute-start | bytes 110600 | tf_op jit(solution)/shard_map/ppermute | solution.py:414
  10.4 0.0 collective-permute-done.1
  10.4 1.0 %collective-permute-done = f32[72,128]{1,0:T(8,128)S(1)} collective-permute-done((f32[72,128]{1,0:T(8,128)S(1)}, f32[72,128]{1,0:T(8,128)S(1)}, u32[]{:S(2)}, u32[]{:S(2)}) %collective-permute-start) | collective-permute-done | bytes 36896 | tf_op jit(solution)/shard_map/ppermute | solution.py:413
  11.4 2.5 %collective-permute-start.5 = (f32[144,128]{1,0:T(8,128)S(1)}, f32[144,128]{1,0:T(8,128)S(1)}, u32[]{:S(2)}, u32[]{:S(2)}) collective-permute-start(f32[144,128]{1,0:T(8,128)S(1)} %pad_maximum_fusion.1.rest_1_), channel_id=1, source_target_pairs={{2,4},{6,0},{4,2},{0,6},{3,5},{7,1},{5,3},{1,7},{10,12},{14,8},{12... | collective-permute-start | bytes 221192 | tf_op jit(solution)/shard_map/ppermute | solution.py:442
  13.9 0.5 %collective-permute-start.4 = (f32[144,128]{1,0:T(8,128)S(1)}, f32[144,128]{1,0:T(8,128)S(1)}, u32[]{:S(2)}, u32[]{:S(2)}) collective-permute-start(f32[144,128]{1,0:T(8,128)S(1)} %pad_maximum_fusion.1.rest_1_), channel_id=1, source_target_pairs={{0,2},{4,6},{2,0},{6,4},{1,3},{5,7},{3,1},{7,5},{8,10},{12,14},{10... | collective-permute-start | bytes 221192 | tf_op jit(solution)/shard_map/ppermute | solution.py:442
  14.4 0.0 collective-permute-done.3.rest_3_
  14.4 0.0 collective-permute-done.2.rest_2_
  14.4 0.1 collective-permute-start.6
  14.5 0.0 copy-start.7
  14.5 0.0 copy-start.9
  14.6 0.0 copy-start.11
  14.6 0.0 copy-start.5
  14.6 0.0 copy-start.6
  14.6 0.0 copy-start.4
  14.6 0.0 copy-start.3
  14.6 0.0 copy-start.1
  14.6 0.0 copy-start.2
  14.7 2.0 %collective-permute-done.5.rest_5_ = f32[144,128]{1,0:T(8,128)S(1)} collective-permute-done((f32[144,128]{1,0:T(8,128)S(1)}, f32[144,128]{1,0:T(8,128)S(1)}, u32[]{:S(2)}, u32[]{:S(2)}) %collective-permute-start.5) | collective-permute-done | bytes 73760 | tf_op jit(solution)/shard_map/ppermute | solution.py:442
  16.7 0.0 collective-permute-start.8
  16.7 1.5 %collective-permute-done.4.rest_4_ = f32[144,128]{1,0:T(8,128)S(1)} collective-permute-done((f32[144,128]{1,0:T(8,128)S(1)}, f32[144,128]{1,0:T(8,128)S(1)}, u32[]{:S(2)}, u32[]{:S(2)}) %collective-permute-start.4) | collective-permute-done | bytes 73760 | tf_op jit(solution)/shard_map/ppermute | solution.py:442
  18.2 0.0 collective-permute-start.7
  18.2 0.1 pad_add_fusion.parities
  18.4 0.6 %copy-done.8 = s32[8]{0:T(128)S(1)} copy-done((s32[8]{0:T(128)S(1)}, s32[8]{0:T(128)}, u32[]{:S(2)}) %copy-start.8) | copy-done | bytes 56
  19.0 0.0 copy-done.10
  19.0 0.8 %prep.1 = (bf16[144,128]{1,0:T(8,128)(2,1)S(1)}, bf16[144,128]{1,0:T(8,128)(2,1)S(1)}, f32[8,128]{1,0:T(8,128)S(1)}, f32[1,128]{1,0:T(1,128)S(1)}, f32[8,256]{1,...) custom-call(s32[3]{0:T(128)S(1)} %pad_add_fusion.parities, ...), custom_call_target="tpu_custom_call" | custom-call | tf_op jit(solution)/shard_map/prep/pallas_call | solution.py:421
  19.8 0.0 collective-permute-done.8.rest_8_
  19.8 0.0 collective-permute-done.7.rest_7_
  19.8 0.0 collective-permute-done.6.rest_6_
  19.8 1.8 %edges.1 = (f32[1,8]{1,0:T(1,128)S(1)}, f32[72,128]{1,0:T(8,128)S(1)}, f32[200,128]{1,0:T(8,128)S(1)}, f32[200,128]{1,0:T(8,128)S(1)}, f32[200,128]{1,0:T(8,128)...) custom-call(bf16[144,128]{1,0:T(8,128)(2,1)S(1)} %get-tuple-element.34.picks_in, ...), custom_call_target="tpu_custom_call" | custom-call | tf_op jit(solution)/shard_map/edges/pallas_call | solution.py:459
  21.6 0.6 %collective-permute-start.10 = (f32[200,128]{1,0:T(8,128)S(1)}, f32[200,128]{1,0:T(8,128)S(1)}, u32[]{:S(2)}, u32[]{:S(2)}) collective-permute-start(f32[200,128]{1,0:T(8,128)S(1)} %get-tuple-element.53), channel_id=1, source_target_pairs={{1,0},{0,1},{3,2},{2,3},{5,4},{4,5},{7,6},{6,7},{9,8},{8,9},{11,10... | collective-permute-start | bytes 307208 | tf_op jit(solution)/shard_map/ppermute | solution.py:484
  22.2 0.1 collective-permute-start.12
  22.3 0.4 %collective-permute-start.9 = (f32[200,128]{1,0:T(8,128)S(1)}, f32[200,128]{1,0:T(8,128)S(1)}, u32[]{:S(2)}, u32[]{:S(2)}) collective-permute-start(f32[200,128]{1,0:T(8,128)S(1)} %get-tuple-element.51), channel_id=1, source_target_pairs={{1,0},{0,1},{3,2},{2,3},{5,4},{4,5},{7,6},{6,7},{9,8},{8,9},{11,10... | collective-permute-start | bytes 307208 | tf_op jit(solution)/shard_map/ppermute | solution.py:484
  22.7 0.4 %collective-permute-done.10 = f32[200,128]{1,0:T(8,128)S(1)} collective-permute-done((f32[200,128]{1,0:T(8,128)S(1)}, f32[200,128]{1,0:T(8,128)S(1)}, u32[]{:S(2)}, u32[]{:S(2)}) %collective-permute-start.10) | collective-permute-done | bytes 102432 | tf_op jit(solution)/shard_map/ppermute | solution.py:484
  23.2 0.9 %collective-permute-start.11 = (f32[200,128]{1,0:T(8,128)S(1)}, f32[200,128]{1,0:T(8,128)S(1)}, u32[]{:S(2)}, u32[]{:S(2)}) collective-permute-start(f32[200,128]{1,0:T(8,128)S(1)} %add.29), channel_id=1, source_target_pairs={{2,0},{6,4},{0,2},{4,6},{3,1},{7,5},{1,3},{5,7},{10,8},{14,12},{8,... | collective-permute-start | bytes 307208 | tf_op jit(solution)/shard_map/ppermute | solution.py:488
  24.0 0.0 collective-permute-done.12
  24.0 1.2 %collective-permute-start.13 = (f32[200,128]{1,0:T(8,128)S(1)}, f32[200,128]{1,0:T(8,128)S(1)}, u32[]{:S(2)}, u32[]{:S(2)}) collective-permute-start(f32[200,128]{1,0:T(8,128)S(1)} %add.31), channel_id=1, source_target_pairs={{4,2},{0,6},{2,4},{6,0},{5,3},{1,7},{3,5},{7,1},{12,10},{8,14},{10... | collective-permute-start | bytes 307208 | tf_op jit(solution)/shard_map/ppermute | solution.py:488
  25.3 0.0 collective-permute-done.9
  25.3 3.7 %collective-permute-done.11 = f32[200,128]{1,0:T(8,128)S(1)} collective-permute-done((f32[200,128]{1,0:T(8,128)S(1)}, f32[200,128]{1,0:T(8,128)S(1)}, u32[]{:S(2)}, u32[]{:S(2)}) %collective-permute-start.11) | collective-permute-done | bytes 102432 | tf_op jit(solution)/shard_map/ppermute | solution.py:488
  29.0 1.5 %collective-permute-done.13 = f32[200,128]{1,0:T(8,128)S(1)} collective-permute-done((f32[200,128]{1,0:T(8,128)S(1)}, f32[200,128]{1,0:T(8,128)S(1)}, u32[]{:S(2)}, u32[]{:S(2)}) %collective-permute-start.13) | collective-permute-done | bytes 102432 | tf_op jit(solution)/shard_map/ppermute | solution.py:488
  30.6 1.9 %collective-permute-start.15 = (f32[72,128]{1,0:T(8,128)S(1)}, f32[72,128]{1,0:T(8,128)S(1)}, u32[]{:S(2)}, u32[]{:S(2)}) collective-permute-start(f32[72,128]{1,0:T(8,128)S(1)} %concatenate.16), channel_id=1, source_target_pairs={{16,8},{0,24},{8,16},{24,0},{17,9},{1,25},{9,17},{25,1},{18,10},{2... | collective-permute-start | bytes 110600 | tf_op jit(solution)/shard_map/ppermute | solution.py:492
  32.5 0.0 collective-permute-start.14
  32.5 4.0 %collective-permute-done.15.rest_2_ = f32[72,128]{1,0:T(8,128)S(1)} collective-permute-done((f32[72,128]{1,0:T(8,128)S(1)}, f32[72,128]{1,0:T(8,128)S(1)}, u32[]{:S(2)}, u32[]{:S(2)}) %collective-permute-start.15) | collective-permute-done | bytes 36896 | tf_op jit(solution)/shard_map/ppermute | solution.py:492
  36.4 0.4 collective-permute-done.14.rest_1_
  36.8 0.8 %finish.1 = (f32[1,8]{1,0:T(1,128)}, f32[3,8]{1,0:T(4,128)}, f32[8,256]{1,0:T(8,128)}, f32[3,8,256]{2,1,0:T(8,128)}) custom-call(f32[1,8]{1,0:T(1,128)S(1)} %get-tuple-element.47.energies_in, f32[72,128]{1,0:T(8,128)S(1)} %get-tuple-element.48.own, f32[8,24]{1,0:T(8,128)S(1)} %get-tuple-element.49.lands, f32[200,128]{1,0:T(8,128)S(1)} %add_add_fusion.rest_0_, ...), custom_call_target="tpu_custom_call" | custom-call | tf_op jit(solution)/shard_map/finish/pallas_call | solution.py:494
  (22 shorter events, 0.1 us)
Async XLA Ops:
  2.3 8.1 %collective-permute-start.1 = (f32[72,128]{1,0:T(8,128)S(1)}, f32[72,128]{1,0:T(8,128)S(1)}, u32[]{:S(2)}, u32[]{:S(2)}) collective-permute-start(f32[72,128]{1,0:T(8,128)S(1)} %pack.1.rest_0_), channel_id=1, source_target_pairs={{8,16},{24,0},{16,8},{0,24},{9,17},{25,1},{17,9},{1,25},{10,18},{2... | collective-permute-start | bytes 110600 | tf_op jit(solution)/shard_map/ppermute | solution.py:413
  7.4 4.0 %collective-permute-start = (f32[72,128]{1,0:T(8,128)S(1)}, f32[72,128]{1,0:T(8,128)S(1)}, u32[]{:S(2)}, u32[]{:S(2)}) collective-permute-start(f32[72,128]{1,0:T(8,128)S(1)} %pack.1.rest_0_), channel_id=1, source_target_pairs={{0,8},{16,24},{8,0},{24,16},{1,9},{17,25},{9,1},{25,17},{2,10},{18... | collective-permute-start | bytes 110600 | tf_op jit(solution)/shard_map/ppermute | solution.py:413
  7.4 7.0 %collective-permute-start.3 = (f32[72,128]{1,0:T(8,128)S(1)}, f32[72,128]{1,0:T(8,128)S(1)}, u32[]{:S(2)}, u32[]{:S(2)}) collective-permute-start(f32[72,128]{1,0:T(8,128)S(1)} %pack.1.rest_0_), channel_id=1, source_target_pairs={{2,4},{6,0},{4,2},{0,6},{3,5},{7,1},{5,3},{1,7},{10,12},{14,8},{12... | collective-permute-start | bytes 110600 | tf_op jit(solution)/shard_map/ppermute | solution.py:414
  9.9 4.6 %collective-permute-start.2 = (f32[72,128]{1,0:T(8,128)S(1)}, f32[72,128]{1,0:T(8,128)S(1)}, u32[]{:S(2)}, u32[]{:S(2)}) collective-permute-start(f32[72,128]{1,0:T(8,128)S(1)} %pack.1.rest_0_), channel_id=1, source_target_pairs={{0,2},{4,6},{2,0},{6,4},{1,3},{5,7},{3,1},{7,5},{8,10},{12,14},{10... | collective-permute-start | bytes 110600 | tf_op jit(solution)/shard_map/ppermute | solution.py:414
  11.4 7.0 %copy-start = (bf16[64,1536]{1,0:T(8,128)(2,1)S(1)}, bf16[64,1536]{1,0:T(8,128)(2,1)}, u32[]{:S(2)}) copy-start(bf16[64,1536]{1,0:T(8,128)(2,1)} %rest_5_.1) | copy-start | bytes 589828
  11.4 5.3 %collective-permute-start.5 = (f32[144,128]{1,0:T(8,128)S(1)}, f32[144,128]{1,0:T(8,128)S(1)}, u32[]{:S(2)}, u32[]{:S(2)}) collective-permute-start(f32[144,128]{1,0:T(8,128)S(1)} %pad_maximum_fusion.1.rest_1_), channel_id=1, source_target_pairs={{2,4},{6,0},{4,2},{0,6},{3,5},{7,1},{5,3},{1,7},{10,12},{14,8},{12... | collective-permute-start | bytes 221192 | tf_op jit(solution)/shard_map/ppermute | solution.py:442
  13.9 4.4 %collective-permute-start.4 = (f32[144,128]{1,0:T(8,128)S(1)}, f32[144,128]{1,0:T(8,128)S(1)}, u32[]{:S(2)}, u32[]{:S(2)}) collective-permute-start(f32[144,128]{1,0:T(8,128)S(1)} %pad_maximum_fusion.1.rest_1_), channel_id=1, source_target_pairs={{0,2},{4,6},{2,0},{6,4},{1,3},{5,7},{3,1},{7,5},{8,10},{12,14},{10... | collective-permute-start | bytes 221192 | tf_op jit(solution)/shard_map/ppermute | solution.py:442
  14.4 5.3 %collective-permute-start.6 = (f32[360,128]{1,0:T(8,128)S(1)}, f32[360,128]{1,0:T(8,128)S(1)}, u32[]{:S(2)}, u32[]{:S(2)}) collective-permute-start(f32[360,128]{1,0:T(8,128)S(1)} %pad_maximum_fusion), channel_id=1, source_target_pairs={{0,1},{1,0},{2,3},{3,2},{4,5},{5,4},{6,7},{7,6},{8,9},{9,8},{10,11... | collective-permute-start | bytes 552968 | tf_op jit(solution)/shard_map/ppermute | solution.py:446
  14.5 3.8 %copy-start.7 = (bf16[8,64]{1,0:T(8,128)(2,1)S(1)}, bf16[8,64]{1,0:T(8,128)(2,1)}, u32[]{:S(2)}) copy-start(bf16[8,64]{1,0:T(8,128)(2,1)} %rest_3_.1) | copy-start | bytes 3076
  14.5 3.8 %copy-start.9 = (f32[256]{0:T(256)S(1)}, f32[256]{0:T(256)}, u32[]{:S(2)}) copy-start(f32[256]{0:T(256)} %param.25) | copy-start | bytes 3076
  14.6 3.8 %copy-start.11 = (s32[8]{0:T(128)S(1)}, s32[8]{0:T(128)}, u32[]{:S(2)}) copy-start(s32[8]{0:T(128)} %param.16) | copy-start | bytes 100
  14.6 3.8 %copy-start.5 = (s32[16,8]{0,1:T(8,128)S(1)}, s32[16,8]{0,1:T(8,128)}, u32[]{:S(2)}) copy-start(s32[16,8]{0,1:T(8,128)} %param.19) | copy-start | bytes 1540
  14.6 3.8 %copy-start.6 = (f32[4,256]{1,0:T(4,128)S(1)}, f32[4,256]{1,0:T(4,128)}, u32[]{:S(2)}) copy-start(f32[4,256]{1,0:T(4,128)} %energy_table.1) | copy-start | bytes 12292
  14.6 3.8 %copy-start.4 = (f32[8,3]{0,1:T(4,128)S(1)}, f32[8,3]{0,1:T(4,128)}, u32[]{:S(2)}) copy-start(f32[8,3]{0,1:T(4,128)} %param.13) | copy-start | bytes 292
  14.6 3.8 %copy-start.3 = (bf16[64,64]{1,0:T(8,128)(2,1)S(1)}, bf16[64,64]{1,0:T(8,128)(2,1)}, u32[]{:S(2)}) copy-start(bf16[64,64]{1,0:T(8,128)(2,1)} %rest_4_.1) | copy-start | bytes 24580
  14.6 3.8 %copy-start.1 = (f32[8,3,256]{2,0,1:T(8,128)S(1)}, f32[8,3,256]{2,0,1:T(8,128)}, u32[]{:S(2)}) copy-start(f32[8,3,256]{2,0,1:T(8,128)} %param.15) | copy-start | bytes 73732
  14.6 3.8 %copy-start.2 = (f32[8,256]{1,0:T(8,128)S(1)}, f32[8,256]{1,0:T(8,128)}, u32[]{:S(2)}) copy-start(f32[8,256]{1,0:T(8,128)} %rest_1_.1) | copy-start | bytes 24580
  16.7 3.1 %collective-permute-start.8 = (f32[144,128]{1,0:T(8,128)S(1)}, f32[144,128]{1,0:T(8,128)S(1)}, u32[]{:S(2)}, u32[]{:S(2)}) collective-permute-start(f32[144,128]{1,0:T(8,128)S(1)} %collective-permute-done.5.rest_5_), channel_id=1, source_target_pairs={{0,1},{1,0},{2,3},{3,2},{4,5},{5,4},{6,7},{7,6},{8,9},{9,8},{10,11... | collective-permute-start | bytes 221192 | tf_op jit(solution)/shard_map/ppermute | solution.py:447
  18.2 1.5 %collective-permute-start.7 = (f32[144,128]{1,0:T(8,128)S(1)}, f32[144,128]{1,0:T(8,128)S(1)}, u32[]{:S(2)}, u32[]{:S(2)}) collective-permute-start(f32[144,128]{1,0:T(8,128)S(1)} %collective-permute-done.4.rest_4_), channel_id=1, source_target_pairs={{0,1},{1,0},{2,3},{3,2},{4,5},{5,4},{6,7},{7,6},{8,9},{9,8},{10,11... | collective-permute-start | bytes 221192 | tf_op jit(solution)/shard_map/ppermute | solution.py:447
  18.3 0.7 %copy-start.8 = (s32[8]{0:T(128)S(1)}, s32[8]{0:T(128)}, u32[]{:S(2)}) copy-start(s32[8]{0:T(128)} %bound_rows_in.1) | copy-start | bytes 100
  18.3 0.7 %copy-start.10 = (s32[8]{0:T(128)S(1)}, s32[8]{0:T(128)}, u32[]{:S(2)}) copy-start(s32[8]{0:T(128)} %param.20) | copy-start | bytes 100
  21.6 1.5 %collective-permute-start.10 = (f32[200,128]{1,0:T(8,128)S(1)}, f32[200,128]{1,0:T(8,128)S(1)}, u32[]{:S(2)}, u32[]{:S(2)}) collective-permute-start(f32[200,128]{1,0:T(8,128)S(1)} %get-tuple-element.53), channel_id=1, source_target_pairs={{1,0},{0,1},{3,2},{2,3},{5,4},{4,5},{7,6},{6,7},{9,8},{8,9},{11,10... | collective-permute-start | bytes 307208 | tf_op jit(solution)/shard_map/ppermute | solution.py:484
  22.2 1.8 %collective-permute-start.12 = (f32[200,128]{1,0:T(8,128)S(1)}, f32[200,128]{1,0:T(8,128)S(1)}, u32[]{:S(2)}, u32[]{:S(2)}) collective-permute-start(f32[200,128]{1,0:T(8,128)S(1)} %get-tuple-element.55), channel_id=1, source_target_pairs={{1,0},{0,1},{3,2},{2,3},{5,4},{4,5},{7,6},{6,7},{9,8},{8,9},{11,10... | collective-permute-start | bytes 307208 | tf_op jit(solution)/shard_map/ppermute | solution.py:484
  22.3 3.0 %collective-permute-start.9 = (f32[200,128]{1,0:T(8,128)S(1)}, f32[200,128]{1,0:T(8,128)S(1)}, u32[]{:S(2)}, u32[]{:S(2)}) collective-permute-start(f32[200,128]{1,0:T(8,128)S(1)} %get-tuple-element.51), channel_id=1, source_target_pairs={{1,0},{0,1},{3,2},{2,3},{5,4},{4,5},{7,6},{6,7},{9,8},{8,9},{11,10... | collective-permute-start | bytes 307208 | tf_op jit(solution)/shard_map/ppermute | solution.py:484
  23.2 5.8 %collective-permute-start.11 = (f32[200,128]{1,0:T(8,128)S(1)}, f32[200,128]{1,0:T(8,128)S(1)}, u32[]{:S(2)}, u32[]{:S(2)}) collective-permute-start(f32[200,128]{1,0:T(8,128)S(1)} %add.29), channel_id=1, source_target_pairs={{2,0},{6,4},{0,2},{4,6},{3,1},{7,5},{1,3},{5,7},{10,8},{14,12},{8,... | collective-permute-start | bytes 307208 | tf_op jit(solution)/shard_map/ppermute | solution.py:488
  24.0 6.5 %collective-permute-start.13 = (f32[200,128]{1,0:T(8,128)S(1)}, f32[200,128]{1,0:T(8,128)S(1)}, u32[]{:S(2)}, u32[]{:S(2)}) collective-permute-start(f32[200,128]{1,0:T(8,128)S(1)} %add.31), channel_id=1, source_target_pairs={{4,2},{0,6},{2,4},{6,0},{5,3},{1,7},{3,5},{7,1},{12,10},{8,14},{10... | collective-permute-start | bytes 307208 | tf_op jit(solution)/shard_map/ppermute | solution.py:488
  30.6 5.9 %collective-permute-start.15 = (f32[72,128]{1,0:T(8,128)S(1)}, f32[72,128]{1,0:T(8,128)S(1)}, u32[]{:S(2)}, u32[]{:S(2)}) collective-permute-start(f32[72,128]{1,0:T(8,128)S(1)} %concatenate.16), channel_id=1, source_target_pairs={{16,8},{0,24},{8,16},{24,0},{17,9},{1,25},{9,17},{25,1},{18,10},{2... | collective-permute-start | bytes 110600 | tf_op jit(solution)/shard_map/ppermute | solution.py:492
  32.5 4.3 %collective-permute-start.14 = (f32[72,128]{1,0:T(8,128)S(1)}, f32[72,128]{1,0:T(8,128)S(1)}, u32[]{:S(2)}, u32[]{:S(2)}) collective-permute-start(f32[72,128]{1,0:T(8,128)S(1)} %pad_maximum_fusion.2), channel_id=1, source_target_pairs={{8,0},{24,16},{0,8},{16,24},{9,1},{25,17},{1,9},{17,25},{10,2},{26... | collective-permute-start | bytes 110600 | tf_op jit(solution)/shard_map/ppermute | solution.py:492

commit v3 on v2

--- a/solution.py
+++ b/solution.py
@@ -59,26 +59,29 @@
     copies = [pltpu.make_async_copy(a, b, sems.at[n]) for n, (a, b) in enumerate(pairs)]
     for copy in copies:
         copy.start()
-    for copy in copies:
-        copy.wait()
     boundary = bound_rows.shape[0]
-    channels = scalars.shape[1]
-    halves = channels // LANES
+    halves = scalars.shape[1] // LANES
     source = lax.broadcasted_iota(jnp.int32, (places.shape[1], LANES), 0)
     lane = lax.broadcasted_iota(jnp.int32, (places.shape[1], LANES), 1)
     moved = jnp.zeros(source.shape, jnp.float32)
+    copies[0].wait()
+    atoms = [bound_rows[slot] for slot in range(boundary)]
+    alive = [jnp.where(slot < bound_count[0], 1.0, 0.0).astype(jnp.float32) for slot in range(boundary)]
     for slot in range(boundary):
-        atom = bound_rows[slot]
-        alive = jnp.where(slot < bound_count[0], 1.0, 0.0).astype(jnp.float32)
-        rows = [scalars[pl.ds(atom, 1), :]] + [vectors[a, pl.ds(atom, 1), :] for a in range(3)]
+        moved = jnp.where((lane == slot) & (source == atoms[slot]), alive[slot], moved)
+    copies[1].wait()
+    spots = joined(dot(thirds(jnp.concatenate([places[...], jnp.zeros((5, source.shape[0]), jnp.float32)], axis=0)),
+                       moved.astype(jnp.bfloat16), (1, 0)), 8)
+    copies[2].wait()
+    copies[3].wait()
+    for slot in range(boundary):
+        rows = [scalars[pl.ds(atoms[slot], 1), :]] + [vectors[a, pl.ds(atoms[slot], 1), :] for a in range(3)]
         for part, row in enumerate(rows):
-            row = row * alive
+            row = row * alive[slot]
             for h in range(halves):
                 at = (part * halves + h) * boundary + slot
                 out[at : at + 1, :] = row[:, h * LANES : (h + 1) * LANES]
-        moved = jnp.where((lane == slot) & (source == atom), alive, moved)
-    spots = dot(places[...], moved, (1, 0), HIGHEST)
-    out[4 * halves * boundary :, :] = jnp.concatenate([spots, jnp.zeros((boundary - 3, LANES), jnp.float32)], axis=0)
+    out[4 * halves * boundary :, :] = spots
 
 
 def prep_kernel(
@@ -146,7 +149,7 @@
     ghosts = rest[:tables]
     energies, own_out = rest[tables : tables + 2]
     grads = rest[tables + 2 : tables + 2 + len(sinks)]
-    table, weights, far, steer, place_rows = rest[tables + 2 + len(sinks) :]
+    weights, far, steer, place_rows = rest[tables + 2 + len(sinks) :]
     halves = channels // LANES
     chunks = 4 * halves
     edges = atoms * slots
@@ -202,29 +205,29 @@
     ).astype(f32).astype(bf16)
     steer[...] = dot(direction.astype(bf16), spread, (0, 0))
 
+    table = []
     for part in range(4):
         for h in range(halves):
-            chunk = part * halves + h
             lanes = slice(h * LANES, (h + 1) * LANES)
             own = scalars[:, lanes] if part == 0 else vectors[part - 1, :, lanes]
-            table[:, chunk * LANES : (chunk + 1) * LANES] = pieces(chunk, own).astype(bf16)
-    far[...] = dot(picks, table[...], (0, 0))
+            table.append(pieces(part * halves + h, own).astype(bf16))
+    far[...] = dot(picks, jnp.concatenate(table, axis=1), (0, 0))
 
     tile = 2 * atoms
     steps = edges // tile
     third_part = jnp.asarray(1.0 / 3.0, bf16)
 
-    def edge_inputs(step, h):
+    def edge_inputs(step, h, kind):
         at = slice(step * tile, (step + 1) * tile)
-        s = far[at, h * LANES : (h + 1) * LANES].astype(bf16)
-        v = [far[at, ((1 + a) * halves + h) * LANES : ((1 + a) * halves + h + 1) * LANES].astype(bf16) for a in range(3)]
-        u = [steer[at, a * LANES : (a + 1) * LANES].astype(bf16) for a in range(3)]
-        w = [weights[at, n * channels + h * LANES : n * channels + (h + 1) * LANES].astype(bf16) for n in range(6)]
+        s = far[at, h * LANES : (h + 1) * LANES].astype(kind)
+        v = [far[at, ((1 + a) * halves + h) * LANES : ((1 + a) * halves + h + 1) * LANES].astype(kind) for a in range(3)]
+        u = [steer[at, a * LANES : (a + 1) * LANES].astype(kind) for a in range(3)]
+        w = [weights[at, n * channels + h * LANES : n * channels + (h + 1) * LANES].astype(kind) for n in range(6)]
         return at, s, v, u, w
 
-    def slopes(step, h):
+    def slopes(step, h, kind):
         at = slice(edges + step * tile, edges + (step + 1) * tile)
-        return [weights[at, n * channels + h * LANES : n * channels + (h + 1) * LANES].astype(bf16) for n in range(6)]
+        return [weights[at, n * channels + h * LANES : n * channels + (h + 1) * LANES].astype(kind) for n in range(6)]
 
     def cross(a, b):
         return [a[1] * b[2] - a[2] * b[1], a[2] * b[0] - a[0] * b[2], a[0] * b[1] - a[1] * b[0]]
@@ -238,14 +241,14 @@
     messages = [[] for _ in range(chunks)]
     for step in range(steps):
         for h in range(halves):
-            at, s, v, u, w = edge_inputs(step, h)
+            at, s, v, u, w = edge_inputs(step, h, f32)
             q = inner(u, v)
             along = w[2] * s + w[5] * q
-            keep = w[3] - w[5] * third_part
+            keep = w[3] - w[5] * third_part.astype(w[5].dtype)
             turned = cross([w[4] * x for x in v], u)
             new = [w[0] * s + w[1] * q] + [along * u[a] + keep * v[a] + turned[a] for a in range(3)]
             for part, value in enumerate(new):
-                messages[part * halves + h].append(value)
+                messages[part * halves + h].append(value.astype(bf16))
     weights[edges:, :] = dot(hidden[:, edges:], third[...], (0, 0))
     centre = lax.broadcasted_iota(jnp.int32, (atoms, edges), 1) % atoms
     mine = (centre == lax.broadcasted_iota(jnp.int32, (atoms, edges), 0)).astype(f32).astype(bf16)
@@ -272,11 +275,11 @@
     pulled = [[(scale * jnp.concatenate([x, x], axis=0)).astype(bf16) for x in c] for c in cotangents]
     for step in range(steps):
         for h in range(halves):
-            at, s, v, u, w = edge_inputs(step, h)
+            at, s, v, u, w = edge_inputs(step, h, bf16)
             cs, *cv = pulled[h]
             q = inner(u, v)
             along = w[2] * s + w[5] * q
-            keep = w[3] - w[5] * third_part
+            keep = w[3] - w[5] * third_part.astype(w[5].dtype)
             d = inner(cv, u)
             turn = cross(u, cv)
             spin = cross(cv, v)
@@ -284,15 +287,15 @@
             ds = cs * w[0] + w[2] * d
             dv = [dq * u[a] + keep * cv[a] + w[4] * turn[a] for a in range(3)]
             du = [dq * v[a] + along * cv[a] + w[4] * spin[a] for a in range(3)]
-            g = slopes(step, h)
+            g = slopes(step, h, bf16)
             stretch = [
                 s * (cs * g[0] + d * g[2]) + q * (cs * g[1] + d * g[5]),
-                inner(cv, v) * (g[3] - g[5] * third_part) + inner(u, spin) * g[4],
+                inner(cv, v) * (g[3] - g[5] * third_part.astype(g[5].dtype)) + inner(u, spin) * g[4],
             ]
             for part, value in enumerate([ds] + dv):
-                dfar[part * halves + h].append(value)
+                dfar[part * halves + h].append(value.astype(bf16))
             for a, value in enumerate(du + stretch):
-                dsteer[a * halves + h].append(value)
+                dsteer[a * halves + h].append(value.astype(bf16))
 
     def put(chunk, value):
         for members, ref in zip(sinks, grads):
@@ -466,7 +469,6 @@
         in_specs=[VMEM] * (12 + len(tables)),
         out_specs=[VMEM] * (2 + len(sinks)),
         scratch_shapes=[
-            pltpu.VMEM((rows, chunks * LANES), jnp.bfloat16),
             pltpu.VMEM((2 * edges, 6 * channels), f32),
             pltpu.VMEM((edges, chunks * LANES), f32),
             pltpu.VMEM((edges, 3 * LANES), f32),

time: 37.8 us -> 37.8 us (level)
  no operation moved by 1% of the time
where the time goes in v3:
time: 37.8 us; the launch traced here: 37.6 us
  starting transfers between devices  16.3 us (43%)
  waiting for transfers between devices  14.6 us (39%)
  Pallas kernels  4.36 us (12%)
  between operations  1.55 us (4%)
  local copies, waits for them, and re-layouts  0.66 us (2%)
    ppermute x2, waiting for transfers between devices, shards(): line = line + lax.ppermute(lines[n + 1], 'gy', inverse(pairs))  5.22 us
    ppermute x2, starting transfers between devices, shards(): beside_x = [lax.ppermute(packet, 'gx', pairs) for pairs in perms['gx']]  5.15 us
    ppermute x2, waiting for transfers between devices, shards(): parts.append(lax.ppermute(value, 'gx', inverse(pairs)))  4.33 us
    ppermute x2, waiting for transfers between devices, shards(): corners = [lax.ppermute(across, 'gy', pairs) for pairs in perms['gy']]  3.58 us
    ppermute x2, starting transfers between devices, shards(): corners = [lax.ppermute(across, 'gy', pairs) for pairs in perms['gy']]  3.05 us
    ppermute x2, starting transfers between devices, shards(): beside_y = [lax.ppermute(packet, 'gy', pairs) for pairs in perms['gy']]  2.98 us
    ppermute x2, starting transfers between devices, shards(): line = line + lax.ppermute(lines[n + 1], 'gy', inverse(pairs))  2.09 us
    pallas_call x1, Pallas kernels, shards(): pl.pallas_call(functools.partial(core_kernel, geometry), out_shape=[jax.S...  1.92 us
  transfers between devices with their start and end apart: 16, of which 8 were waited for; matrix products, arithmetic and copies ran while one was open for 0% of the time, Pallas kernels for 2%

profile of v3, /device:TPU:0, one launch (start us, length us, event | category | flops | bytes accessed | tf_op | source)
XLA Modules:
  0.0 37.6 jit_solution(6704333932128857053)
XLA Ops:
  1.3 0.9 %pack.1.rest_0_ = f32[72,128]{1,0:T(8,128)S(1)} custom-call(s32[1]{0:T(128)} %copy.17.bound_count, s32[8]{0:T(128)} %bound_rows_in.1, f32[3,8]{1,0:T(4,128)} %bitcast.17, f32[8,256]{1,0:T(8,128)} %rest_1_.1, f32[3,8,256]{2,1,0:T(8,128)} %bitcast.15), custom_call_target="tpu_custom_call" | custom-call | tf_op jit(solution)/shard_map/pack/pallas_call | solution.py:396
  2.2 5.1 %collective-permute-start.1 = (f32[72,128]{1,0:T(8,128)S(1)}, f32[72,128]{1,0:T(8,128)S(1)}, u32[]{:S(2)}, u32[]{:S(2)}) collective-permute-start(f32[72,128]{1,0:T(8,128)S(1)} %pack.1.rest_0_), channel_id=1, source_target_pairs={{8,16},{24,0},{16,8},{0,24},{9,17},{25,1},{17,9},{1,25},{10,18},{2... | collective-permute-start | bytes 110600 | tf_op jit(solution)/shard_map/ppermute | solution.py:416
  7.3 0.0 collective-permute-start
  7.3 2.4 %collective-permute-start.3 = (f32[72,128]{1,0:T(8,128)S(1)}, f32[72,128]{1,0:T(8,128)S(1)}, u32[]{:S(2)}, u32[]{:S(2)}) collective-permute-start(f32[72,128]{1,0:T(8,128)S(1)} %pack.1.rest_0_), channel_id=1, source_target_pairs={{2,4},{6,0},{4,2},{0,6},{3,5},{7,1},{5,3},{1,7},{10,12},{14,8},{12... | collective-permute-start | bytes 110600 | tf_op jit(solution)/shard_map/ppermute | solution.py:417
  9.8 0.5 %collective-permute-start.2 = (f32[72,128]{1,0:T(8,128)S(1)}, f32[72,128]{1,0:T(8,128)S(1)}, u32[]{:S(2)}, u32[]{:S(2)}) collective-permute-start(f32[72,128]{1,0:T(8,128)S(1)} %pack.1.rest_0_), channel_id=1, source_target_pairs={{0,2},{4,6},{2,0},{6,4},{1,3},{5,7},{3,1},{7,5},{8,10},{12,14},{10... | collective-permute-start | bytes 110600 | tf_op jit(solution)/shard_map/ppermute | solution.py:417
  10.3 0.0 collective-permute-done.1
  10.3 1.0 %collective-permute-done = f32[72,128]{1,0:T(8,128)S(1)} collective-permute-done((f32[72,128]{1,0:T(8,128)S(1)}, f32[72,128]{1,0:T(8,128)S(1)}, u32[]{:S(2)}, u32[]{:S(2)}) %collective-permute-start) | collective-permute-done | bytes 36896 | tf_op jit(solution)/shard_map/ppermute | solution.py:416
  11.3 2.5 %collective-permute-start.5 = (f32[144,128]{1,0:T(8,128)S(1)}, f32[144,128]{1,0:T(8,128)S(1)}, u32[]{:S(2)}, u32[]{:S(2)}) collective-permute-start(f32[144,128]{1,0:T(8,128)S(1)} %pad_maximum_fusion.1.rest_1_), channel_id=1, source_target_pairs={{2,4},{6,0},{4,2},{0,6},{3,5},{7,1},{5,3},{1,7},{10,12},{14,8},{12... | collective-permute-start | bytes 221192 | tf_op jit(solution)/shard_map/ppermute | solution.py:445
  13.8 0.5 %collective-permute-start.4 = (f32[144,128]{1,0:T(8,128)S(1)}, f32[144,128]{1,0:T(8,128)S(1)}, u32[]{:S(2)}, u32[]{:S(2)}) collective-permute-start(f32[144,128]{1,0:T(8,128)S(1)} %pad_maximum_fusion.1.rest_1_), channel_id=1, source_target_pairs={{0,2},{4,6},{2,0},{6,4},{1,3},{5,7},{3,1},{7,5},{8,10},{12,14},{10... | collective-permute-start | bytes 221192 | tf_op jit(solution)/shard_map/ppermute | solution.py:445
  14.3 0.0 collective-permute-done.3.rest_3_
  14.3 0.0 collective-permute-done.2.rest_2_
  14.3 0.1 collective-permute-start.6
  14.4 0.0 copy-start.7
  14.4 0.0 copy-start.9
  14.5 0.0 copy-start.11
  14.5 0.0 copy-start.5
  14.5 0.0 copy-start.6
  14.5 0.0 copy-start.4
  14.5 0.0 copy-start.3
  14.5 0.0 copy-start.1
  14.6 0.0 copy-start.2
  14.6 2.0 %collective-permute-done.5.rest_5_ = f32[144,128]{1,0:T(8,128)S(1)} collective-permute-done((f32[144,128]{1,0:T(8,128)S(1)}, f32[144,128]{1,0:T(8,128)S(1)}, u32[]{:S(2)}, u32[]{:S(2)}) %collective-permute-start.5) | collective-permute-done | bytes 73760 | tf_op jit(solution)/shard_map/ppermute | solution.py:445
  16.6 0.0 collective-permute-start.8
  16.6 1.5 %collective-permute-done.4.rest_4_ = f32[144,128]{1,0:T(8,128)S(1)} collective-permute-done((f32[144,128]{1,0:T(8,128)S(1)}, f32[144,128]{1,0:T(8,128)S(1)}, u32[]{:S(2)}, u32[]{:S(2)}) %collective-permute-start.4) | collective-permute-done | bytes 73760 | tf_op jit(solution)/shard_map/ppermute | solution.py:445
  18.1 0.0 collective-permute-start.7
  18.1 0.1 pad_add_fusion.parities
  18.3 0.6 %copy-done.8 = s32[8]{0:T(128)S(1)} copy-done((s32[8]{0:T(128)S(1)}, s32[8]{0:T(128)}, u32[]{:S(2)}) %copy-start.8) | copy-done | bytes 56
  18.9 0.0 copy-done.10
  18.9 0.8 %prep.1 = (bf16[144,128]{1,0:T(8,128)(2,1)S(1)}, bf16[144,128]{1,0:T(8,128)(2,1)S(1)}, f32[8,128]{1,0:T(8,128)S(1)}, f32[1,128]{1,0:T(1,128)S(1)}, f32[8,256]{1,...) custom-call(s32[3]{0:T(128)S(1)} %pad_add_fusion.parities, ...), custom_call_target="tpu_custom_call" | custom-call | tf_op jit(solution)/shard_map/prep/pallas_call | solution.py:424
  19.7 0.0 collective-permute-done.8.rest_8_
  19.7 0.0 collective-permute-done.7.rest_7_
  19.7 0.0 collective-permute-done.6.rest_6_
  19.7 1.9 %edges.1 = (f32[1,8]{1,0:T(1,128)S(1)}, f32[72,128]{1,0:T(8,128)S(1)}, f32[200,128]{1,0:T(8,128)S(1)}, f32[200,128]{1,0:T(8,128)S(1)}, f32[200,128]{1,0:T(8,128)...) custom-call(bf16[144,128]{1,0:T(8,128)(2,1)S(1)} %get-tuple-element.34.picks_in, ...), custom_call_target="tpu_custom_call" | custom-call | tf_op jit(solution)/shard_map/edges/pallas_call | solution.py:462
  21.6 0.6 %collective-permute-start.10 = (f32[200,128]{1,0:T(8,128)S(1)}, f32[200,128]{1,0:T(8,128)S(1)}, u32[]{:S(2)}, u32[]{:S(2)}) collective-permute-start(f32[200,128]{1,0:T(8,128)S(1)} %get-tuple-element.53), channel_id=1, source_target_pairs={{1,0},{0,1},{3,2},{2,3},{5,4},{4,5},{7,6},{6,7},{9,8},{8,9},{11,10... | collective-permute-start | bytes 307208 | tf_op jit(solution)/shard_map/ppermute | solution.py:486
  22.2 0.1 collective-permute-start.12
  22.3 0.4 %collective-permute-start.9 = (f32[200,128]{1,0:T(8,128)S(1)}, f32[200,128]{1,0:T(8,128)S(1)}, u32[]{:S(2)}, u32[]{:S(2)}) collective-permute-start(f32[200,128]{1,0:T(8,128)S(1)} %get-tuple-element.51), channel_id=1, source_target_pairs={{1,0},{0,1},{3,2},{2,3},{5,4},{4,5},{7,6},{6,7},{9,8},{8,9},{11,10... | collective-permute-start | bytes 307208 | tf_op jit(solution)/shard_map/ppermute | solution.py:486
  22.7 0.4 %collective-permute-done.10 = f32[200,128]{1,0:T(8,128)S(1)} collective-permute-done((f32[200,128]{1,0:T(8,128)S(1)}, f32[200,128]{1,0:T(8,128)S(1)}, u32[]{:S(2)}, u32[]{:S(2)}) %collective-permute-start.10) | collective-permute-done | bytes 102432 | tf_op jit(solution)/shard_map/ppermute | solution.py:486
  23.2 0.8 %collective-permute-start.11 = (f32[200,128]{1,0:T(8,128)S(1)}, f32[200,128]{1,0:T(8,128)S(1)}, u32[]{:S(2)}, u32[]{:S(2)}) collective-permute-start(f32[200,128]{1,0:T(8,128)S(1)} %add.29), channel_id=1, source_target_pairs={{2,0},{6,4},{0,2},{4,6},{3,1},{7,5},{1,3},{5,7},{10,8},{14,12},{8,... | collective-permute-start | bytes 307208 | tf_op jit(solution)/shard_map/ppermute | solution.py:490
  24.0 0.0 collective-permute-done.12
  24.0 1.2 %collective-permute-start.13 = (f32[200,128]{1,0:T(8,128)S(1)}, f32[200,128]{1,0:T(8,128)S(1)}, u32[]{:S(2)}, u32[]{:S(2)}) collective-permute-start(f32[200,128]{1,0:T(8,128)S(1)} %add.31), channel_id=1, source_target_pairs={{4,2},{0,6},{2,4},{6,0},{5,3},{1,7},{3,5},{7,1},{12,10},{8,14},{10... | collective-permute-start | bytes 307208 | tf_op jit(solution)/shard_map/ppermute | solution.py:490
  25.3 0.0 collective-permute-done.9
  25.3 3.7 %collective-permute-done.11 = f32[200,128]{1,0:T(8,128)S(1)} collective-permute-done((f32[200,128]{1,0:T(8,128)S(1)}, f32[200,128]{1,0:T(8,128)S(1)}, u32[]{:S(2)}, u32[]{:S(2)}) %collective-permute-start.11) | collective-permute-done | bytes 102432 | tf_op jit(solution)/shard_map/ppermute | solution.py:490
  29.0 1.5 %collective-permute-done.13 = f32[200,128]{1,0:T(8,128)S(1)} collective-permute-done((f32[200,128]{1,0:T(8,128)S(1)}, f32[200,128]{1,0:T(8,128)S(1)}, u32[]{:S(2)}, u32[]{:S(2)}) %collective-permute-start.13) | collective-permute-done | bytes 102432 | tf_op jit(solution)/shard_map/ppermute | solution.py:490
  30.6 1.9 %collective-permute-start.15 = (f32[72,128]{1,0:T(8,128)S(1)}, f32[72,128]{1,0:T(8,128)S(1)}, u32[]{:S(2)}, u32[]{:S(2)}) collective-permute-start(f32[72,128]{1,0:T(8,128)S(1)} %concatenate.16), channel_id=1, source_target_pairs={{16,8},{0,24},{8,16},{24,0},{17,9},{1,25},{9,17},{25,1},{18,10},{2... | collective-permute-start | bytes 110600 | tf_op jit(solution)/shard_map/ppermute | solution.py:494
  32.4 0.0 collective-permute-start.14
  32.4 4.0 %collective-permute-done.15.rest_2_ = f32[72,128]{1,0:T(8,128)S(1)} collective-permute-done((f32[72,128]{1,0:T(8,128)S(1)}, f32[72,128]{1,0:T(8,128)S(1)}, u32[]{:S(2)}, u32[]{:S(2)}) %collective-permute-start.15) | collective-permute-done | bytes 36896 | tf_op jit(solution)/shard_map/ppermute | solution.py:494
  36.4 0.4 collective-permute-done.14.rest_1_
  36.8 0.8 %finish.1 = (f32[1,8]{1,0:T(1,128)}, f32[3,8]{1,0:T(4,128)}, f32[8,256]{1,0:T(8,128)}, f32[3,8,256]{2,1,0:T(8,128)}) custom-call(f32[1,8]{1,0:T(1,128)S(1)} %get-tuple-element.47.energies_in, f32[72,128]{1,0:T(8,128)S(1)} %get-tuple-element.48.own, f32[8,24]{1,0:T(8,128)S(1)} %get-tuple-element.49.lands, f32[200,128]{1,0:T(8,128)S(1)} %add_add_fusion.rest_0_, ...), custom_call_target="tpu_custom_call" | custom-call | tf_op jit(solution)/shard_map/finish/pallas_call | solution.py:496
  (22 shorter events, 0.1 us)
Async XLA Ops:
  2.2 8.1 %collective-permute-start.1 = (f32[72,128]{1,0:T(8,128)S(1)}, f32[72,128]{1,0:T(8,128)S(1)}, u32[]{:S(2)}, u32[]{:S(2)}) collective-permute-start(f32[72,128]{1,0:T(8,128)S(1)} %pack.1.rest_0_), channel_id=1, source_target_pairs={{8,16},{24,0},{16,8},{0,24},{9,17},{25,1},{17,9},{1,25},{10,18},{2... | collective-permute-start | bytes 110600 | tf_op jit(solution)/shard_map/ppermute | solution.py:416
  7.3 4.0 %collective-permute-start = (f32[72,128]{1,0:T(8,128)S(1)}, f32[72,128]{1,0:T(8,128)S(1)}, u32[]{:S(2)}, u32[]{:S(2)}) collective-permute-start(f32[72,128]{1,0:T(8,128)S(1)} %pack.1.rest_0_), channel_id=1, source_target_pairs={{0,8},{16,24},{8,0},{24,16},{1,9},{17,25},{9,1},{25,17},{2,10},{18... | collective-permute-start | bytes 110600 | tf_op jit(solution)/shard_map/ppermute | solution.py:416
  7.3 7.0 %collective-permute-start.3 = (f32[72,128]{1,0:T(8,128)S(1)}, f32[72,128]{1,0:T(8,128)S(1)}, u32[]{:S(2)}, u32[]{:S(2)}) collective-permute-start(f32[72,128]{1,0:T(8,128)S(1)} %pack.1.rest_0_), channel_id=1, source_target_pairs={{2,4},{6,0},{4,2},{0,6},{3,5},{7,1},{5,3},{1,7},{10,12},{14,8},{12... | collective-permute-start | bytes 110600 | tf_op jit(solution)/shard_map/ppermute | solution.py:417
  9.8 4.6 %collective-permute-start.2 = (f32[72,128]{1,0:T(8,128)S(1)}, f32[72,128]{1,0:T(8,128)S(1)}, u32[]{:S(2)}, u32[]{:S(2)}) collective-permute-start(f32[72,128]{1,0:T(8,128)S(1)} %pack.1.rest_0_), channel_id=1, source_target_pairs={{0,2},{4,6},{2,0},{6,4},{1,3},{5,7},{3,1},{7,5},{8,10},{12,14},{10... | collective-permute-start | bytes 110600 | tf_op jit(solution)/shard_map/ppermute | solution.py:417
  11.3 7.0 %copy-start = (bf16[64,1536]{1,0:T(8,128)(2,1)S(1)}, bf16[64,1536]{1,0:T(8,128)(2,1)}, u32[]{:S(2)}) copy-start(bf16[64,1536]{1,0:T(8,128)(2,1)} %rest_5_.1) | copy-start | bytes 589828
  11.3 5.3 %collective-permute-start.5 = (f32[144,128]{1,0:T(8,128)S(1)}, f32[144,128]{1,0:T(8,128)S(1)}, u32[]{:S(2)}, u32[]{:S(2)}) collective-permute-start(f32[144,128]{1,0:T(8,128)S(1)} %pad_maximum_fusion.1.rest_1_), channel_id=1, source_target_pairs={{2,4},{6,0},{4,2},{0,6},{3,5},{7,1},{5,3},{1,7},{10,12},{14,8},{12... | collective-permute-start | bytes 221192 | tf_op jit(solution)/shard_map/ppermute | solution.py:445
  13.8 4.4 %collective-permute-start.4 = (f32[144,128]{1,0:T(8,128)S(1)}, f32[144,128]{1,0:T(8,128)S(1)}, u32[]{:S(2)}, u32[]{:S(2)}) collective-permute-start(f32[144,128]{1,0:T(8,128)S(1)} %pad_maximum_fusion.1.rest_1_), channel_id=1, source_target_pairs={{0,2},{4,6},{2,0},{6,4},{1,3},{5,7},{3,1},{7,5},{8,10},{12,14},{10... | collective-permute-start | bytes 221192 | tf_op jit(solution)/shard_map/ppermute | solution.py:445
  14.3 5.3 %collective-permute-start.6 = (f32[360,128]{1,0:T(8,128)S(1)}, f32[360,128]{1,0:T(8,128)S(1)}, u32[]{:S(2)}, u32[]{:S(2)}) collective-permute-start(f32[360,128]{1,0:T(8,128)S(1)} %pad_maximum_fusion), channel_id=1, source_target_pairs={{0,1},{1,0},{2,3},{3,2},{4,5},{5,4},{6,7},{7,6},{8,9},{9,8},{10,11... | collective-permute-start | bytes 552968 | tf_op jit(solution)/shard_map/ppermute | solution.py:449
  14.4 3.8 %copy-start.7 = (bf16[8,64]{1,0:T(8,128)(2,1)S(1)}, bf16[8,64]{1,0:T(8,128)(2,1)}, u32[]{:S(2)}) copy-start(bf16[8,64]{1,0:T(8,128)(2,1)} %rest_3_.1) | copy-start | bytes 3076
  14.4 3.8 %copy-start.9 = (f32[256]{0:T(256)S(1)}, f32[256]{0:T(256)}, u32[]{:S(2)}) copy-start(f32[256]{0:T(256)} %param.25) | copy-start | bytes 3076
  14.5 3.8 %copy-start.11 = (s32[8]{0:T(128)S(1)}, s32[8]{0:T(128)}, u32[]{:S(2)}) copy-start(s32[8]{0:T(128)} %param.16) | copy-start | bytes 100
  14.5 3.8 %copy-start.5 = (s32[16,8]{0,1:T(8,128)S(1)}, s32[16,8]{0,1:T(8,128)}, u32[]{:S(2)}) copy-start(s32[16,8]{0,1:T(8,128)} %param.19) | copy-start | bytes 1540
  14.5 3.8 %copy-start.6 = (f32[4,256]{1,0:T(4,128)S(1)}, f32[4,256]{1,0:T(4,128)}, u32[]{:S(2)}) copy-start(f32[4,256]{1,0:T(4,128)} %energy_table.1) | copy-start | bytes 12292
  14.5 3.8 %copy-start.4 = (f32[8,3]{0,1:T(4,128)S(1)}, f32[8,3]{0,1:T(4,128)}, u32[]{:S(2)}) copy-start(f32[8,3]{0,1:T(4,128)} %param.13) | copy-start | bytes 292
  14.5 3.8 %copy-start.3 = (bf16[64,64]{1,0:T(8,128)(2,1)S(1)}, bf16[64,64]{1,0:T(8,128)(2,1)}, u32[]{:S(2)}) copy-start(bf16[64,64]{1,0:T(8,128)(2,1)} %rest_4_.1) | copy-start | bytes 24580
  14.5 3.8 %copy-start.1 = (f32[8,3,256]{2,0,1:T(8,128)S(1)}, f32[8,3,256]{2,0,1:T(8,128)}, u32[]{:S(2)}) copy-start(f32[8,3,256]{2,0,1:T(8,128)} %param.15) | copy-start | bytes 73732
  14.6 3.8 %copy-start.2 = (f32[8,256]{1,0:T(8,128)S(1)}, f32[8,256]{1,0:T(8,128)}, u32[]{:S(2)}) copy-start(f32[8,256]{1,0:T(8,128)} %rest_1_.1) | copy-start | bytes 24580
  16.6 3.1 %collective-permute-start.8 = (f32[144,128]{1,0:T(8,128)S(1)}, f32[144,128]{1,0:T(8,128)S(1)}, u32[]{:S(2)}, u32[]{:S(2)}) collective-permute-start(f32[144,128]{1,0:T(8,128)S(1)} %collective-permute-done.5.rest_5_), channel_id=1, source_target_pairs={{0,1},{1,0},{2,3},{3,2},{4,5},{5,4},{6,7},{7,6},{8,9},{9,8},{10,11... | collective-permute-start | bytes 221192 | tf_op jit(solution)/shard_map/ppermute | solution.py:450
  18.1 1.5 %collective-permute-start.7 = (f32[144,128]{1,0:T(8,128)S(1)}, f32[144,128]{1,0:T(8,128)S(1)}, u32[]{:S(2)}, u32[]{:S(2)}) collective-permute-start(f32[144,128]{1,0:T(8,128)S(1)} %collective-permute-done.4.rest_4_), channel_id=1, source_target_pairs={{0,1},{1,0},{2,3},{3,2},{4,5},{5,4},{6,7},{7,6},{8,9},{9,8},{10,11... | collective-permute-start | bytes 221192 | tf_op jit(solution)/shard_map/ppermute | solution.py:450
  18.2 0.7 %copy-start.8 = (s32[8]{0:T(128)S(1)}, s32[8]{0:T(128)}, u32[]{:S(2)}) copy-start(s32[8]{0:T(128)} %bound_rows_in.1) | copy-start | bytes 100
  18.2 0.7 %copy-start.10 = (s32[8]{0:T(128)S(1)}, s32[8]{0:T(128)}, u32[]{:S(2)}) copy-start(s32[8]{0:T(128)} %param.20) | copy-start | bytes 100
  21.6 1.5 %collective-permute-start.10 = (f32[200,128]{1,0:T(8,128)S(1)}, f32[200,128]{1,0:T(8,128)S(1)}, u32[]{:S(2)}, u32[]{:S(2)}) collective-permute-start(f32[200,128]{1,0:T(8,128)S(1)} %get-tuple-element.53), channel_id=1, source_target_pairs={{1,0},{0,1},{3,2},{2,3},{5,4},{4,5},{7,6},{6,7},{9,8},{8,9},{11,10... | collective-permute-start | bytes 307208 | tf_op jit(solution)/shard_map/ppermute | solution.py:486
  22.2 1.8 %collective-permute-start.12 = (f32[200,128]{1,0:T(8,128)S(1)}, f32[200,128]{1,0:T(8,128)S(1)}, u32[]{:S(2)}, u32[]{:S(2)}) collective-permute-start(f32[200,128]{1,0:T(8,128)S(1)} %get-tuple-element.55), channel_id=1, source_target_pairs={{1,0},{0,1},{3,2},{2,3},{5,4},{4,5},{7,6},{6,7},{9,8},{8,9},{11,10... | collective-permute-start | bytes 307208 | tf_op jit(solution)/shard_map/ppermute | solution.py:486
  22.3 3.0 %collective-permute-start.9 = (f32[200,128]{1,0:T(8,128)S(1)}, f32[200,128]{1,0:T(8,128)S(1)}, u32[]{:S(2)}, u32[]{:S(2)}) collective-permute-start(f32[200,128]{1,0:T(8,128)S(1)} %get-tuple-element.51), channel_id=1, source_target_pairs={{1,0},{0,1},{3,2},{2,3},{5,4},{4,5},{7,6},{6,7},{9,8},{8,9},{11,10... | collective-permute-start | bytes 307208 | tf_op jit(solution)/shard_map/ppermute | solution.py:486
  23.2 5.8 %collective-permute-start.11 = (f32[200,128]{1,0:T(8,128)S(1)}, f32[200,128]{1,0:T(8,128)S(1)}, u32[]{:S(2)}, u32[]{:S(2)}) collective-permute-start(f32[200,128]{1,0:T(8,128)S(1)} %add.29), channel_id=1, source_target_pairs={{2,0},{6,4},{0,2},{4,6},{3,1},{7,5},{1,3},{5,7},{10,8},{14,12},{8,... | collective-permute-start | bytes 307208 | tf_op jit(solution)/shard_map/ppermute | solution.py:490
  24.0 6.5 %collective-permute-start.13 = (f32[200,128]{1,0:T(8,128)S(1)}, f32[200,128]{1,0:T(8,128)S(1)}, u32[]{:S(2)}, u32[]{:S(2)}) collective-permute-start(f32[200,128]{1,0:T(8,128)S(1)} %add.31), channel_id=1, source_target_pairs={{4,2},{0,6},{2,4},{6,0},{5,3},{1,7},{3,5},{7,1},{12,10},{8,14},{10... | collective-permute-start | bytes 307208 | tf_op jit(solution)/shard_map/ppermute | solution.py:490
  30.6 5.9 %collective-permute-start.15 = (f32[72,128]{1,0:T(8,128)S(1)}, f32[72,128]{1,0:T(8,128)S(1)}, u32[]{:S(2)}, u32[]{:S(2)}) collective-permute-start(f32[72,128]{1,0:T(8,128)S(1)} %concatenate.16), channel_id=1, source_target_pairs={{16,8},{0,24},{8,16},{24,0},{17,9},{1,25},{9,17},{25,1},{18,10},{2... | collective-permute-start | bytes 110600 | tf_op jit(solution)/shard_map/ppermute | solution.py:494
  32.4 4.3 %collective-permute-start.14 = (f32[72,128]{1,0:T(8,128)S(1)}, f32[72,128]{1,0:T(8,128)S(1)}, u32[]{:S(2)}, u32[]{:S(2)}) collective-permute-start(f32[72,128]{1,0:T(8,128)S(1)} %pad_maximum_fusion.2), channel_id=1, source_target_pairs={{8,0},{24,16},{0,8},{16,24},{9,1},{25,17},{1,9},{17,25},{10,2},{26... | collective-permute-start | bytes 110600 | tf_op jit(solution)/shard_map/ppermute | solution.py:494
